TPU v7x, 32 devices: a whole 2x2x4 slice. The times are simulated.
32 devices in a mesh: seq: 16 (over z, y, core), head: 2 (over x).
Axes of the slice: x: 2, y: 2, z: 4, core: 2. Of those that a mesh axis runs over, the one named last changes fastest.
Arguments:
- queries: bfloat16 [8192, 4096], P(('seq', 'head')), may hold values from -64 to 64
- keys: bfloat16 [8192, 1024], P(('seq', 'head')), may hold values from -6 to 6
- values: bfloat16 [8192, 1024], P(('seq', 'head')), may hold values from -6 to 6
- level_bias: float32 [32, 4], P('head'), may hold values from -1 to 2
- anchor_bias: float32 [32], P('head'), may hold values from 1 to 4
- partners: int32 [16, 4], P('seq'), may hold values from 0 to 15, as said below
- anchor_positions: int32 [64], replicated, may hold values from 0 to 8191, as said below
Outputs:
- attended: bfloat16 [8192, 4096], P(('seq', 'head'))
Inputs may be any that keep to these rules, and one draw needn't show every extreme that they name: `partners`: row b holds b XOR 2**j once for each j of 0 to 3, in an order drawn for each block. `anchor_positions`: distinct positions.
All inputs are finite; a program needn't handle non-finite values.
Results may differ from a plain program's by a relative error of at most 0.0045.
Values may be sent and summed in bfloat16 or wider, within the bound.
A program may use at most 192 MiB of HBM per device.

v0:
```python
import jax
import jax.numpy as jnp
from jax import lax
from jax.sharding import PartitionSpec as P

HD = 128


def partner_2(value, axis, stride):
    return lax.ppermute(value, axis, [(i, i ^ 1 << stride) for i in range(lax.axis_size(axis))])


def absorb(softmax_state, query_heads, key_block, value_block, score_bias, score_scale):
    running_max, running_sum, weighted = softmax_state
    kv_local = query_heads.shape[1]
    head_dim = query_heads.shape[3]
    key_heads = key_block.reshape(key_block.shape[0], kv_local, head_dim)
    value_heads = value_block.reshape(value_block.shape[0], kv_local, head_dim)
    scores = jnp.einsum(
        "tkgd,skd->kgts", query_heads, key_heads, preferred_element_type=jnp.float32
    )
    scores = scores * score_scale + score_bias[:, :, None, None]
    new_max = jnp.maximum(running_max, jnp.max(scores, axis=-1))
    rescale = jnp.exp(running_max - new_max)
    weights = jnp.exp(scores - new_max[..., None])
    running_sum = running_sum * rescale + jnp.sum(weights, axis=-1)
    update = jnp.einsum(
        "kgts,skd->kgtd",
        weights.astype(jnp.bfloat16),
        value_heads,
        preferred_element_type=jnp.float32,
    )
    weighted = weighted * rescale[..., None] + update
    return (new_max, running_sum, weighted)


def on_device(queries, keys, values, level_bias, anchor_bias, partners, anchor_positions):
    query_rows, key_rows, value_rows = (
        lax.all_to_all(queries, "head", split_axis=1, concat_axis=0, tiled=True),
        lax.all_to_all(keys, "head", split_axis=1, concat_axis=0, tiled=True),
        lax.all_to_all(values, "head", split_axis=1, concat_axis=0, tiled=True),
    )
    block_rows = query_rows.shape[0]
    head_dim = HD
    kv_local = key_rows.shape[1] // head_dim
    group_size = level_bias.shape[0] // kv_local
    score_scale = head_dim ** (-0.5)
    query_heads = query_rows.reshape(block_rows, kv_local, group_size, head_dim)
    block_index = lax.axis_index("seq")
    level_count = lax.axis_size("seq").bit_length() - 1
    token_index = block_index * block_rows + jnp.arange(block_rows, dtype=jnp.int32)
    selector = (anchor_positions[:, None] == token_index[None, :]).astype(jnp.bfloat16)
    anchor_keys = jnp.dot(selector, key_rows, preferred_element_type=jnp.float32)
    anchor_vals = jnp.dot(selector, value_rows, preferred_element_type=jnp.float32)
    initial = (
        jnp.full((kv_local, group_size, block_rows), -jnp.inf, jnp.float32),
        jnp.zeros((kv_local, group_size, block_rows), jnp.float32),
        jnp.zeros((kv_local, group_size, block_rows, head_dim), jnp.float32),
    )
    own_bias = jnp.zeros((kv_local, group_size), jnp.float32)
    softmax_state = absorb(initial, query_heads, key_rows, value_rows, own_bias, score_scale)
    bit_list = list(range(level_count))
    carried_keys = anchor_keys.astype(jnp.bfloat16)
    carried_vals = anchor_vals.astype(jnp.bfloat16)
    for bit_level in bit_list:
        partner_keys, partner_vals, more_keys, more_vals = partner_2(
            (key_rows, value_rows, carried_keys, carried_vals), "seq", bit_level
        )
        carried_keys = (carried_keys.astype(jnp.float32) + more_keys.astype(jnp.float32)).astype(
            jnp.bfloat16
        )
        carried_vals = (carried_vals.astype(jnp.float32) + more_vals.astype(jnp.float32)).astype(
            jnp.bfloat16
        )
        partner = jnp.bitwise_xor(block_index, 1 << bit_level)
        chosen = (partners[0] == partner).astype(jnp.float32)
        softmax_state = absorb(
            softmax_state,
            query_heads,
            partner_keys,
            partner_vals,
            jnp.sum(level_bias * chosen[None, :], axis=1).reshape(kv_local, group_size),
            score_scale,
        )
    softmax_state = absorb(
        softmax_state,
        query_heads,
        carried_keys,
        carried_vals,
        anchor_bias.reshape(kv_local, group_size),
        score_scale,
    )
    running_max, running_sum, weighted = softmax_state
    result = (
        (weighted / running_sum[..., None])
        .transpose(2, 0, 1, 3)
        .reshape(block_rows, -1)
        .astype(jnp.bfloat16)
    )
    return lax.all_to_all(result, "head", split_axis=0, concat_axis=1, tiled=True)


def solution(mesh):
    in_specs = (
        P(("seq", "head"), None),
        P(("seq", "head"), None),
        P(("seq", "head"), None),
        P("head", None),
        P("head"),
        P("seq", None),
        P(),
    )
    out_specs = P(("seq", "head"), None)
    return jax.shard_map(
        on_device, mesh=mesh, in_specs=in_specs, out_specs=out_specs, check_vma=False
    )
```

profile of v0, /device:TPU:0, one launch (start us, length us, event | category | flops | bytes accessed | tf_op | source)
XLA Modules:
  0.0 284.3 jit_solution(17350575310486674656)
XLA Ops:
  0.0 2.1 copy.48
  2.1 4.2 %all-to-all-start = ((bf16[256,2,512]{0,2,1:T(8,128)(2,1)}), bf16[256,2,512]{0,2,1:T(8,128)(2,1)S(1)}, u32[]{:S(2)}, u32[]{:S(2)}) async-start(bf16[256,2,512]{0,2,1:T(8,128)(2,1)} %bitcast), calls=%async_computation | async-start | bytes 1048576 | tf_op jit(solution)/shard_map/all_to_all | solution.py:40
  6.3 2.0 copy.53
  8.4 6.7 %all-to-all-done = bf16[256,2,512]{0,2,1:T(8,128)(2,1)S(1)} async-done(((bf16[256,2,512]{0,2,1:T(8,128)(2,1)}), bf16[256,2,512]{0,2,1:T(8,128)(2,1)S(1)}, u32[]{:S(2)}, u32[]{:S(2)}) %all-to-all-start) | async-done | bytes 524320 | tf_op jit(solution)/shard_map/all_to_all | solution.py:40
  15.0 3.5 %all-to-all-start.2 = ((bf16[256,2,512]{0,2,1:T(8,128)(2,1)}), bf16[256,2,512]{0,2,1:T(8,128)(2,1)S(1)}, u32[]{:S(2)}, u32[]{:S(2)}) async-start(bf16[256,2,512]{0,2,1:T(8,128)(2,1)} %bitcast.6), calls=%async_computation.2 | async-start | bytes 1048576 | tf_op jit(solution)/shard_map/all_to_all | solution.py:41
  18.6 3.2 %copy.168 = bf16[32,2,8,2048]{3,2,0,1:T(8,128)(2,1)} copy(bf16[32,2,8,2048]{3,2,1,0:T(8,128)(2,1)} %bitcast.288) | data formatting | bytes 4194304 | tf_op jit(solution)/shard_map/all_to_all | solution.py:39
  22.0 2.9 %collective-permute-start.6 = (bf16[512,512]{1,0:T(8,128)(2,1)S(1)}, bf16[512,512]{1,0:T(8,128)(2,1)}, u32[]{:S(2)}, u32[]{:S(2)}) collective-permute-start(bf16[512,512]{1,0:T(8,128)(2,1)S(1)} %bitcast.274), channel_id=1, source_target_pairs={{0,16},{2,18},{4,20},{6,22},{8,24},{10,26},{12,28},{14,30},{16,0},... | collective-permute-start | bytes 1572872 | tf_op jit(solution)/shard_map/ppermute | solution.py:10
  24.9 1.6 collective-permute-start.4
  26.5 0.9 convolution_convert_fusion.1
  27.5 3.8 %all-to-all-start.1 = ((bf16[256,2,2048]{2,0,1:T(8,128)(2,1)}), bf16[256,2,2048]{2,0,1:T(8,128)(2,1)S(1)}, u32[]{:S(2)}, u32[]{:S(2)}) async-start(bf16[256,2,2048]{2,0,1:T(8,128)(2,1)} %bitcast.258), calls=%async_computation.1 | async-start | bytes 4194304 | tf_op jit(solution)/shard_map/all_to_all | solution.py:39
  31.3 1.3 copy.54
  32.5 0.9 convolution_convert_fusion
  34.0 1.6 collective-permute-start.9
  35.6 0.9 collective-permute-start.13
  36.5 2.1 collective-permute-done.9
  39.2 0.8 collective-permute-done.13
  40.0 0.9 collective-permute-start.14
  40.8 9.7 %collective-permute-done.10 = bf16[64,512]{1,0:T(8,128)(2,1)S(1)} collective-permute-done((bf16[64,512]{1,0:T(8,128)(2,1)S(1)}, bf16[64,512]{1,0:T(8,128)(2,1)S(1)}, u32[]{:S(2)}, u32[]{:S(2)}) %collective-permute-start.10) | collective-permute-done | bytes 65568 | tf_op jit(solution)/shard_map/ppermute | solution.py:10
  50.6 1.8 collective-permute-start.11
  52.4 1.3 collective-permute-start.15
  53.7 0.7 add.198
  54.3 3.7 %collective-permute-done.11 = bf16[64,512]{1,0:T(8,128)(2,1)S(1)} collective-permute-done((bf16[64,512]{1,0:T(8,128)(2,1)S(1)}, bf16[64,512]{1,0:T(8,128)(2,1)S(1)}, u32[]{:S(2)}, u32[]{:S(2)}) %collective-permute-start.11) | collective-permute-done | bytes 65568 | tf_op jit(solution)/shard_map/ppermute | solution.py:10
  58.1 1.6 collective-permute-start.2
  59.6 1.4 collective-permute-start.3
  61.3 3.0 %collective-permute-start.7 = (bf16[512,512]{1,0:T(8,128)(2,1)S(1)}, bf16[512,512]{1,0:T(8,128)(2,1)}, u32[]{:S(2)}, u32[]{:S(2)}) collective-permute-start(bf16[512,512]{1,0:T(8,128)(2,1)S(1)} %bitcast.282), channel_id=1, source_target_pairs={{0,16},{2,18},{4,20},{6,22},{8,24},{10,26},{12,28},{14,30},{16,0},... | collective-permute-start | bytes 1572872 | tf_op jit(solution)/shard_map/ppermute | solution.py:10
  64.6 0.9 reshape.203
  65.6 0.9 reshape.205
  66.6 2.1 copy.58
  68.7 2.1 copy.77
  70.7 2.1 copy.71
  73.0 1.3 copy.65
  74.2 2.1 copy.62
  76.3 3.3 %collective-permute-done.3 = bf16[512,512]{1,0:T(8,128)(2,1)} collective-permute-done((bf16[512,512]{1,0:T(8,128)(2,1)S(1)}, bf16[512,512]{1,0:T(8,128)(2,1)}, u32[]{:S(2)}, u32[]{:S(2)}) %collective-permute-start.3) | collective-permute-done | bytes 524320 | tf_op jit(solution)/shard_map/ppermute | solution.py:10
  79.6 2.0 copy.68
  81.6 4.6 %collective-permute-done.5 = bf16[512,512]{1,0:T(8,128)(2,1)} collective-permute-done((bf16[512,512]{1,0:T(8,128)(2,1)S(1)}, bf16[512,512]{1,0:T(8,128)(2,1)}, u32[]{:S(2)}, u32[]{:S(2)}) %collective-permute-start.5) | collective-permute-done | bytes 524320 | tf_op jit(solution)/shard_map/ppermute | solution.py:10
  86.2 2.1 copy.74
  88.3 2.1 copy.80
  90.4 1.3 copy-done.1
  91.7 3.5 %reshape.204 = bf16[512,4,4,128]{3,2,1,0:T(4,128)(2,1)S(1)} reshape(bf16[2,256,2048]{2,1,0:T(8,128)(2,1)} %bitcast.270) | data formatting | bytes 4194304 | tf_op jit(solution)/shard_map/reshape | solution.py:48
  95.2 8.1 %bitcast_reduce_fusion.4 = (f32[4,4,512]{2,1,0:T(4,128)S(1)}, f32[4,512,512,4]{2,1,3,0:T(8,128)}) fusion(bf16[512,4,4,128]{3,2,1,0:T(4,128)(2,1)S(1)} %reshape.204, bf16[512,4,128,1]{2,1,0,3:T(4,128)(2,1)} %bitcast.283), kind=kOutput, calls=%fused_computation.13 | convolution fusion | flops 1082122240 | bytes 19431424 | tf_op jit(solution)/shard_map/tkgd,skd->kgts/dot_general | solution.py:19
  103.4 3.3 %bitcast_reduce_fusion.5 = (f32[4,4,512]{2,1,0:T(4,128)S(1)}, f32[4,64,512,4]{2,1,3,0:T(8,128)}) fusion(f32[4,4]{1,0:T(4,128)} %add.198, bf16[512,4,4,128]{3,2,1,0:T(4,128)(2,1)S(1)} %reshape.204, bf16[64,4,128,1]{2,1,0,3:T(4,128)(2,1)S(1)} %bitcast.305), kind=kOutput, calls=%fused_computation.51 | convolution fusion | flops 135782400 | bytes 4292672 | tf_op jit(solution)/shard_map/tkgd,skd->kgts/dot_general | solution.py:19
  106.7 7.5 %bitcast_reduce_fusion.3 = (f32[4,4,512]{2,1,0:T(4,128)S(1)}, f32[4,512,512,4]{2,1,3,0:T(8,128)}) fusion(f32[4,4]{1,0:T(4,128)S(1)} %add.172, bf16[512,4,128,1]{0,2,3,1:T(8,128)(2,1)S(1)} %bitcast.287, bf16[512,4,4,128]{3,2,1,0:T(4,128)(2,1)S(1)} %reshape.204), kind=kOutput, calls=%fused_computation.10 | convolution fusion | flops 1086316544 | bytes 19431488 | tf_op jit(solution)/shard_map/tkgd,skd->kgts/dot_general | solution.py:19
  114.2 7.5 %bitcast_reduce_fusion = (f32[4,4,512]{2,1,0:T(4,128)S(1)}, f32[4,512,512,4]{2,1,3,0:T(8,128)}) fusion(f32[4,4]{1,0:T(4,128)S(1)} %add.187, bf16[512,4,128,1]{0,2,3,1:T(8,128)(2,1)S(1)} %bitcast.285, bf16[512,4,4,128]{3,2,1,0:T(4,128)(2,1)S(1)} %reshape.204), kind=kOutput, calls=%fused_computation.1 | convolution fusion | flops 1086316544 | bytes 19431488 | tf_op jit(solution)/shard_map/tkgd,skd->kgts/dot_general | solution.py:19
  121.7 7.5 %bitcast_reduce_fusion.1 = (f32[4,4,512]{2,1,0:T(4,128)S(1)}, f32[4,512,512,4]{2,1,3,0:T(8,128)}) fusion(f32[4,4]{1,0:T(4,128)S(1)} %add.182, bf16[512,4,128,1]{0,2,3,1:T(8,128)(2,1)S(1)} %bitcast.284, bf16[512,4,4,128]{3,2,1,0:T(4,128)(2,1)S(1)} %reshape.204), kind=kOutput, calls=%fused_computation.4 | convolution fusion | flops 1086316544 | bytes 19431488 | tf_op jit(solution)/shard_map/tkgd,skd->kgts/dot_general | solution.py:19
  129.3 8.0 %bitcast_reduce_fusion.2 = (f32[4,4,512]{2,1,0:T(4,128)S(1)}, f32[4,512,512,4]{2,1,3,0:T(8,128)}) fusion(f32[4,4]{1,0:T(4,128)S(1)} %add.177, bf16[512,4,128,1]{0,2,3,1:T(8,128)(2,1)S(1)} %bitcast.286, bf16[512,4,4,128]{3,2,1,0:T(4,128)(2,1)S(1)} %reshape.204), kind=kOutput, calls=%fused_computation.7 | convolution fusion | flops 1086316544 | bytes 19431488 | tf_op jit(solution)/shard_map/tkgd,skd->kgts/dot_general | solution.py:19
  137.3 8.5 %fusion.5 = f32[4,4,512]{2,1,0:T(4,128)S(1)} fusion(f32[4,512,512,4]{2,1,3,0:T(8,128)} %get-tuple-element.35, f32[4,4,512]{2,1,0:T(4,128)S(1)} %get-tuple-element.34), kind=kLoop, calls=%fused_computation.19 | loop fusion | flops 12574720 | bytes 16842752 | tf_op jit(solution)/shard_map/reduce_sum | solution.py:26
  145.8 0.6 fusion.73
  146.5 0.6 fusion.87
  147.1 12.2 %fusion.25 = f32[4,4,512,128]{3,2,1,0:T(8,128)} fusion(bf16[512,4,128,1]{0,2,3,1:T(8,128)(2,1)S(1)} %bitcast.297, f32[4,512,512,4]{2,1,3,0:T(8,128)} %get-tuple-element.37, f32[4,4,512]{2,1,0:T(4,128)S(1)} %bitcast.312, f32[4,4]{1,0:T(4,128)S(1)} %add.172), kind=kOutput, calls=%fused_computation.35 | convolution fusion | flops 1090519040 | bytes 21528640 | tf_op jit(solution)/shard_map/kgts,skd->kgtd/dot_general | solution.py:27
  159.3 13.8 %fusion.7 = (f32[4,4,512]{2,1,0:T(4,128)S(1)}, f32[4,4,512]{2,1,0:T(4,128)}) fusion(f32[4,512,512,4]{2,1,3,0:T(8,128)} %get-tuple-element.37, f32[4,4,512]{2,1,0:T(4,128)S(1)} %bitcast.313, f32[4,4]{1,0:T(4,128)S(1)} %add.172, f32[4,4,512]{2,1,0:T(4,128)S(1)} %bitcast.310, f32[4,4]{1,0:T(4,128)S(1)} %add.177, f32[4,512,512,4]{2,1,3,0:T(8,128)} %get-tuple-element.33), kind=kLoop, calls=%fused_computation.21 | loop fusion | flops 33538048 | bytes 33685632 | tf_op jit(solution)/shard_map/reduce_sum | solution.py:26
  173.1 12.4 %fusion.23 = f32[4,4,512,128]{3,2,1,0:T(8,128)} fusion(bf16[512,4,128,1]{0,2,3,1:T(8,128)(2,1)S(1)} %bitcast.296, f32[4,512,512,4]{2,1,3,0:T(8,128)} %get-tuple-element.33, f32[4,4,512]{2,1,0:T(4,128)S(1)} %bitcast.311, f32[4,4]{1,0:T(4,128)S(1)} %add.177), kind=kOutput, calls=%fused_computation.34 | convolution fusion | flops 1090519040 | bytes 21528640 | tf_op jit(solution)/shard_map/kgts,skd->kgtd/dot_general | solution.py:27
  185.5 0.5 fusion.37
  186.1 3.1 %fusion.39 = f32[4,4,512,128]{3,2,1,0:T(8,128)} fusion(f32[4,64,512,4]{2,1,3,0:T(8,128)S(1)} %copy-done, f32[4,4,512]{2,1,0:T(4,128)S(1)} %bitcast.299, f32[4,4]{1,0:T(4,128)S(1)} %copy-done.16, bf16[64,4,128,1]{2,1,0,3:T(4,128)(2,1)S(1)} %bitcast.304), kind=kOutput, calls=%fused_computation.58 | convolution fusion | flops 136314880 | bytes 6389824 | tf_op jit(solution)/shard_map/kgts,skd->kgtd/dot_general | solution.py:27
  189.2 11.7 %fusion.15 = f32[4,4,512,128]{3,2,1,0:T(8,128)} fusion(f32[4,512,512,4]{2,1,3,0:T(8,128)} %get-tuple-element.35, f32[4,4,512]{2,1,0:T(4,128)S(1)} %get-tuple-element.34, bf16[512,4,128,1]{2,1,0,3:T(4,128)(2,1)S(1)} %bitcast.291), kind=kOutput, calls=%fused_computation.29 | convolution fusion | flops 1086324736 | bytes 21528576 | tf_op jit(solution)/shard_map/kgts,skd->kgtd/dot_general | solution.py:27
  200.9 12.4 %fusion.21 = f32[4,4,512,128]{3,2,1,0:T(8,128)} fusion(bf16[512,4,128,1]{0,2,3,1:T(8,128)(2,1)S(1)} %bitcast.295, f32[4,512,512,4]{2,1,3,0:T(8,128)} %get-tuple-element.31, f32[4,4,512]{2,1,0:T(4,128)} %bitcast.308, f32[4,4]{1,0:T(4,128)S(1)} %add.182), kind=kOutput, calls=%fused_computation.33 | convolution fusion | flops 1090519040 | bytes 21528640 | tf_op jit(solution)/shard_map/kgts,skd->kgtd/dot_general | solution.py:27
  213.4 13.9 %fusion.11 = (f32[4,4,512]{2,1,0:T(4,128)S(1)}, f32[4,4,512]{2,1,0:T(4,128)S(1)}) fusion(f32[4,512,512,4]{2,1,3,0:T(8,128)} %get-tuple-element.31, f32[4,4,512]{2,1,0:T(4,128)S(1)} %bitcast.309, f32[4,4]{1,0:T(4,128)S(1)} %add.182, f32[4,4,512]{2,1,0:T(4,128)S(1)} %bitcast.306, f32[4,4]{1,0:T(4,128)S(1)} %add.187, f32[4,512,512,4]{2,1,3,0:T(8,128)} %get-tuple-element.29), kind=kLoop, calls=%fused_computation.25 | loop fusion | flops 33538048 | bytes 33685632 | tf_op jit(solution)/shard_map/reduce_sum | solution.py:26
  227.8 1.2 copy-done.22
  229.0 1.2 copy-done.23
  230.2 14.3 %fusion.28 = bf16[512,4,4,128]{3,0,2,1:T(8,128)(2,1)S(1)} fusion(f32[4,4,512,128]{3,2,1,0:T(8,128)S(1)} %copy-done.2, f32[4,4,512,128]{3,2,1,0:T(8,128)S(1)} %copy-done.23, f32[4,4,512,128]{3,2,1,0:T(8,128)S(1)} %copy-done.22, f32[4,4,512,128]{3,2,1,0:T(8,128)S(1)} %copy-done.21, f32[4,4,512,128]{3,2,1,0:T(8,128)S(1)} %copy-done.3, ...), kind=kOutput, calls=%fused_computation.38 | convolution fusion | flops 1104150528 | bytes 40632384 | tf_op jit(solution)/shard_map/kgts,skd->kgtd/dot_general | solution.py:27
  244.4 1.6 copy.86
  246.1 2.8 convert_element_type.145
  248.9 28.6 %all_to_all.70 = bf16[2,256,2048]{2,1,0:T(8,128)(2,1)S(1)} all-to-all(bf16[2,256,2048]{2,1,0:T(8,128)(2,1)} %convert_element_type.145), channel_id=1, replica_groups=mesh['seq'=16,'head'=2] {'head'}, dimensions={0} | all-to-all | bytes 4194304 | tf_op jit(solution)/shard_map/all_to_all | solution.py:100
  277.5 2.5 copy.87
  280.0 4.1 %copy.88 = bf16[256,4096]{1,0:T(8,128)(2,1)} copy(bf16[256,4096]{0,1:T(8,128)(2,1)} %bitcast.272) | data formatting | bytes 4194304 | tf_op jit(solution)/shard_map/all_to_all | solution.py:100
  (82 shorter events, 2.9 us)
Async XLA Ops:
  0.0 53.7 %copy-start.19 = (s32[1,4]{1,0:T(1,128)S(1)}, s32[1,4]{1,0:T(1,128)}, u32[]{:S(2)}) copy-start(s32[1,4]{1,0:T(1,128)} %param.12) | copy-start | bytes 52
  0.0 53.7 %copy-start.20 = (f32[16]{0:T(128)S(1)}, f32[16]{0:T(128)}, u32[]{:S(2)}) copy-start(f32[16]{0:T(128)} %param.11) | copy-start | bytes 196
  0.0 64.2 %copy-start.18 = (f32[16,4]{0,1:T(4,128)S(1)}, f32[16,4]{0,1:T(4,128)}, u32[]{:S(2)}) copy-start(f32[16,4]{0,1:T(4,128)} %param.10) | copy-start | bytes 772
  2.1 13.0 %all-to-all-start = ((bf16[256,2,512]{0,2,1:T(8,128)(2,1)}), bf16[256,2,512]{0,2,1:T(8,128)(2,1)S(1)}, u32[]{:S(2)}, u32[]{:S(2)}) async-start(bf16[256,2,512]{0,2,1:T(8,128)(2,1)} %bitcast), calls=%async_computation | async-start | bytes 1048576 | tf_op jit(solution)/shard_map/all_to_all | solution.py:40
  15.0 12.4 %all-to-all-start.2 = ((bf16[256,2,512]{0,2,1:T(8,128)(2,1)}), bf16[256,2,512]{0,2,1:T(8,128)(2,1)S(1)}, u32[]{:S(2)}, u32[]{:S(2)}) async-start(bf16[256,2,512]{0,2,1:T(8,128)(2,1)} %bitcast.6), calls=%async_computation.2 | async-start | bytes 1048576 | tf_op jit(solution)/shard_map/all_to_all | solution.py:41
  21.9 37.7 %collective-permute-start = (bf16[512,512]{1,0:T(8,128)(2,1)S(1)}, bf16[512,512]{1,0:T(8,128)(2,1)}, u32[]{:S(2)}, u32[]{:S(2)}) collective-permute-start(bf16[512,512]{1,0:T(8,128)(2,1)S(1)} %bitcast.273), channel_id=1, source_target_pairs={{0,2},{2,0},{4,6},{6,4},{8,10},{10,8},{12,14},{14,12},{16,18},{18,... | collective-permute-start | bytes 1572872 | tf_op jit(solution)/shard_map/ppermute | solution.py:10
  22.0 39.1 %collective-permute-start.6 = (bf16[512,512]{1,0:T(8,128)(2,1)S(1)}, bf16[512,512]{1,0:T(8,128)(2,1)}, u32[]{:S(2)}, u32[]{:S(2)}) collective-permute-start(bf16[512,512]{1,0:T(8,128)(2,1)S(1)} %bitcast.274), channel_id=1, source_target_pairs={{0,16},{2,18},{4,20},{6,22},{8,24},{10,26},{12,28},{14,30},{16,0},... | collective-permute-start | bytes 1572872 | tf_op jit(solution)/shard_map/ppermute | solution.py:10
  24.9 36.3 %collective-permute-start.4 = (bf16[512,512]{1,0:T(8,128)(2,1)S(1)}, bf16[512,512]{1,0:T(8,128)(2,1)}, u32[]{:S(2)}, u32[]{:S(2)}) collective-permute-start(bf16[512,512]{1,0:T(8,128)(2,1)S(1)} %bitcast.275), channel_id=1, source_target_pairs={{0,8},{2,10},{4,12},{6,14},{8,0},{10,2},{12,4},{14,6},{16,24},{18,... | collective-permute-start | bytes 1572872 | tf_op jit(solution)/shard_map/ppermute | solution.py:10
  27.4 6.6 %collective-permute-start.8 = (bf16[64,512]{1,0:T(8,128)(2,1)S(1)}, bf16[64,512]{1,0:T(8,128)(2,1)S(1)}, u32[]{:S(2)}, u32[]{:S(2)}) collective-permute-start(bf16[64,512]{1,0:T(8,128)(2,1)S(1)} %convolution_convert_fusion.1), channel_id=1, source_target_pairs={{0,2},{2,0},{4,6},{6,4},{8,10},{10,8},{12,14},{14,12},{16,18},{18,... | collective-permute-start | bytes 196616 | tf_op jit(solution)/shard_map/ppermute | solution.py:10
  27.5 3.8 %copy-start.7 = (bf16[256,2,512]{0,2,1:T(8,128)(2,1)}, bf16[256,2,512]{0,2,1:T(8,128)(2,1)S(1)}, u32[]{:S(2)}) copy-start(bf16[256,2,512]{0,2,1:T(8,128)(2,1)S(1)} %all-to-all-done.2) | copy-start | bytes 1572868
  27.5 62.9 %all-to-all-start.1 = ((bf16[256,2,2048]{2,0,1:T(8,128)(2,1)}), bf16[256,2,2048]{2,0,1:T(8,128)(2,1)S(1)}, u32[]{:S(2)}, u32[]{:S(2)}) async-start(bf16[256,2,2048]{2,0,1:T(8,128)(2,1)} %bitcast.258), calls=%async_computation.1 | async-start | bytes 4194304 | tf_op jit(solution)/shard_map/all_to_all | solution.py:39
  33.4 2.2 collective-permute-start.12
  34.0 4.6 %collective-permute-start.9 = (bf16[64,512]{1,0:T(8,128)(2,1)S(1)}, bf16[64,512]{1,0:T(8,128)(2,1)S(1)}, u32[]{:S(2)}, u32[]{:S(2)}) collective-permute-start(bf16[64,512]{1,0:T(8,128)(2,1)S(1)} %add_convert_fusion.7), channel_id=1, source_target_pairs={{0,4},{2,6},{4,0},{6,2},{8,12},{10,14},{12,8},{14,10},{16,20},{18,... | collective-permute-start | bytes 196616 | tf_op jit(solution)/shard_map/ppermute | solution.py:10
  35.6 4.3 %collective-permute-start.13 = (bf16[64,512]{1,0:T(8,128)(2,1)S(1)}, bf16[64,512]{1,0:T(8,128)(2,1)S(1)}, u32[]{:S(2)}, u32[]{:S(2)}) collective-permute-start(bf16[64,512]{1,0:T(8,128)(2,1)S(1)} %add_convert_fusion.3), channel_id=1, source_target_pairs={{0,4},{2,6},{4,0},{6,2},{8,12},{10,14},{12,8},{14,10},{16,20},{18,... | collective-permute-start | bytes 196616 | tf_op jit(solution)/shard_map/ppermute | solution.py:10
  38.7 11.9 %collective-permute-start.10 = (bf16[64,512]{1,0:T(8,128)(2,1)S(1)}, bf16[64,512]{1,0:T(8,128)(2,1)S(1)}, u32[]{:S(2)}, u32[]{:S(2)}) collective-permute-start(bf16[64,512]{1,0:T(8,128)(2,1)S(1)} %add_convert_fusion.6), channel_id=1, source_target_pairs={{0,8},{2,10},{4,12},{6,14},{8,0},{10,2},{12,4},{14,6},{16,24},{18,... | collective-permute-start | bytes 196616 | tf_op jit(solution)/shard_map/ppermute | solution.py:10
  40.0 12.4 %collective-permute-start.14 = (bf16[64,512]{1,0:T(8,128)(2,1)S(1)}, bf16[64,512]{1,0:T(8,128)(2,1)S(1)}, u32[]{:S(2)}, u32[]{:S(2)}) collective-permute-start(bf16[64,512]{1,0:T(8,128)(2,1)S(1)} %add_convert_fusion.2), channel_id=1, source_target_pairs={{0,8},{2,10},{4,12},{6,14},{8,0},{10,2},{12,4},{14,6},{16,24},{18,... | collective-permute-start | bytes 196616 | tf_op jit(solution)/shard_map/ppermute | solution.py:10
  50.6 7.5 %collective-permute-start.11 = (bf16[64,512]{1,0:T(8,128)(2,1)S(1)}, bf16[64,512]{1,0:T(8,128)(2,1)S(1)}, u32[]{:S(2)}, u32[]{:S(2)}) collective-permute-start(bf16[64,512]{1,0:T(8,128)(2,1)S(1)} %add_convert_fusion.5), channel_id=1, source_target_pairs={{0,16},{2,18},{4,20},{6,22},{8,24},{10,26},{12,28},{14,30},{16,0},... | collective-permute-start | bytes 196616 | tf_op jit(solution)/shard_map/ppermute | solution.py:10
  52.4 7.2 %collective-permute-start.15 = (bf16[64,512]{1,0:T(8,128)(2,1)S(1)}, bf16[64,512]{1,0:T(8,128)(2,1)S(1)}, u32[]{:S(2)}, u32[]{:S(2)}) collective-permute-start(bf16[64,512]{1,0:T(8,128)(2,1)S(1)} %add_convert_fusion.1), channel_id=1, source_target_pairs={{0,16},{2,18},{4,20},{6,22},{8,24},{10,26},{12,28},{14,30},{16,0},... | collective-permute-start | bytes 196616 | tf_op jit(solution)/shard_map/ppermute | solution.py:10
  58.1 14.9 %collective-permute-start.2 = (bf16[512,512]{1,0:T(8,128)(2,1)S(1)}, bf16[512,512]{1,0:T(8,128)(2,1)}, u32[]{:S(2)}, u32[]{:S(2)}) collective-permute-start(bf16[512,512]{1,0:T(8,128)(2,1)S(1)} %bitcast.277), channel_id=1, source_target_pairs={{0,4},{2,6},{4,0},{6,2},{8,12},{10,14},{12,8},{14,10},{16,20},{18,... | collective-permute-start | bytes 1572872 | tf_op jit(solution)/shard_map/ppermute | solution.py:10
  59.6 14.6 %collective-permute-start.1 = (bf16[512,512]{1,0:T(8,128)(2,1)S(1)}, bf16[512,512]{1,0:T(8,128)(2,1)}, u32[]{:S(2)}, u32[]{:S(2)}) collective-permute-start(bf16[512,512]{1,0:T(8,128)(2,1)S(1)} %bitcast.279), channel_id=1, source_target_pairs={{0,2},{2,0},{4,6},{6,4},{8,10},{10,8},{12,14},{14,12},{16,18},{18,... | collective-permute-start | bytes 1572872 | tf_op jit(solution)/shard_map/ppermute | solution.py:10
  59.6 19.9 %collective-permute-start.3 = (bf16[512,512]{1,0:T(8,128)(2,1)S(1)}, bf16[512,512]{1,0:T(8,128)(2,1)}, u32[]{:S(2)}, u32[]{:S(2)}) collective-permute-start(bf16[512,512]{1,0:T(8,128)(2,1)S(1)} %bitcast.280), channel_id=1, source_target_pairs={{0,4},{2,6},{4,0},{6,2},{8,12},{10,14},{12,8},{14,10},{16,20},{18,... | collective-permute-start | bytes 1572872 | tf_op jit(solution)/shard_map/ppermute | solution.py:10
  61.1 25.2 %collective-permute-start.5 = (bf16[512,512]{1,0:T(8,128)(2,1)S(1)}, bf16[512,512]{1,0:T(8,128)(2,1)}, u32[]{:S(2)}, u32[]{:S(2)}) collective-permute-start(bf16[512,512]{1,0:T(8,128)(2,1)S(1)} %bitcast.281), channel_id=1, source_target_pairs={{0,8},{2,10},{4,12},{6,14},{8,0},{10,2},{12,4},{14,6},{16,24},{18,... | collective-permute-start | bytes 1572872 | tf_op jit(solution)/shard_map/ppermute | solution.py:10
  61.3 27.1 %collective-permute-start.7 = (bf16[512,512]{1,0:T(8,128)(2,1)S(1)}, bf16[512,512]{1,0:T(8,128)(2,1)}, u32[]{:S(2)}, u32[]{:S(2)}) collective-permute-start(bf16[512,512]{1,0:T(8,128)(2,1)S(1)} %bitcast.282), channel_id=1, source_target_pairs={{0,16},{2,18},{4,20},{6,22},{8,24},{10,26},{12,28},{14,30},{16,0},... | collective-permute-start | bytes 1572872 | tf_op jit(solution)/shard_map/ppermute | solution.py:10
  88.3 18.3 %copy-start.6 = (bf16[512,512]{0,1:T(8,128)(2,1)S(1)}, bf16[512,512]{0,1:T(8,128)(2,1)}, u32[]{:S(2)}) copy-start(bf16[512,512]{0,1:T(8,128)(2,1)} %copy.58) | copy-start | bytes 1572868
  90.4 1.3 copy-start.1
  95.2 19.0 %copy-start.5 = (bf16[512,512]{0,1:T(8,128)(2,1)S(1)}, bf16[512,512]{0,1:T(8,128)(2,1)}, u32[]{:S(2)}) copy-start(bf16[512,512]{0,1:T(8,128)(2,1)} %copy.77) | copy-start | bytes 1572868
  106.7 15.1 %copy-start.4 = (bf16[512,512]{0,1:T(8,128)(2,1)S(1)}, bf16[512,512]{0,1:T(8,128)(2,1)}, u32[]{:S(2)}) copy-start(bf16[512,512]{0,1:T(8,128)(2,1)} %copy.71) | copy-start | bytes 1572868
  129.2 17.8 %copy-start.12 = (bf16[512,512]{0,1:T(8,128)(2,1)S(1)}, bf16[512,512]{0,1:T(8,128)(2,1)}, u32[]{:S(2)}) copy-start(bf16[512,512]{0,1:T(8,128)(2,1)} %copy.62) | copy-start | bytes 1572868
  159.3 13.8 %copy-start.11 = (bf16[512,512]{0,1:T(8,128)(2,1)S(1)}, bf16[512,512]{0,1:T(8,128)(2,1)}, u32[]{:S(2)}) copy-start(bf16[512,512]{0,1:T(8,128)(2,1)} %copy.68) | copy-start | bytes 1572868
  173.1 12.4 %copy-start = (f32[4,64,512,4]{2,1,3,0:T(8,128)S(1)}, f32[4,64,512,4]{2,1,3,0:T(8,128)}, u32[]{:S(2)}) copy-start(f32[4,64,512,4]{2,1,3,0:T(8,128)} %get-tuple-element.27) | copy-start | bytes 6291460
  173.1 12.4 %copy-start.16 = (f32[4,4]{1,0:T(4,128)S(1)}, f32[4,4]{1,0:T(4,128)}, u32[]{:S(2)}) copy-start(f32[4,4]{1,0:T(4,128)} %add.198) | copy-start | bytes 196
  173.1 16.1 %copy-start.8 = (bf16[512,4,128]{2,1,0:T(4,128)(2,1)S(1)}, bf16[512,4,128]{2,1,0:T(4,128)(2,1)}, u32[]{:S(2)}) copy-start(bf16[512,4,128]{2,1,0:T(4,128)(2,1)} %reshape.205) | copy-start | bytes 1572868
  185.5 15.4 %copy-start.10 = (bf16[512,512]{0,1:T(8,128)(2,1)S(1)}, bf16[512,512]{0,1:T(8,128)(2,1)}, u32[]{:S(2)}) copy-start(bf16[512,512]{0,1:T(8,128)(2,1)} %copy.74) | copy-start | bytes 1572868
  189.2 24.1 %copy-start.14 = (f32[2,8,512]{2,1,0:T(8,128)S(1)}, f32[2,8,512]{2,1,0:T(8,128)}, u32[]{:S(2)}) copy-start(f32[2,8,512]{2,1,0:T(8,128)} %get-tuple-element.43) | copy-start | bytes 98308
  189.2 24.1 %copy-start.15 = (f32[2,8,512]{2,1,0:T(8,128)S(1)}, f32[2,8,512]{2,1,0:T(8,128)}, u32[]{:S(2)}) copy-start(f32[2,8,512]{2,1,0:T(8,128)} %get-tuple-element.44) | copy-start | bytes 98308
  213.3 14.0 %copy-start.13 = (f32[4,4,512]{2,1,0:T(4,128)S(1)}, f32[4,4,512]{2,1,0:T(4,128)}, u32[]{:S(2)}) copy-start(f32[4,4,512]{2,1,0:T(4,128)} %get-tuple-element.39) | copy-start | bytes 98308
  213.3 14.1 %copy-start.2 = (f32[4,4,512,128]{3,2,1,0:T(8,128)S(1)}, f32[4,4,512,128]{3,2,1,0:T(8,128)}, u32[]{:S(2)}) copy-start(f32[4,4,512,128]{3,2,1,0:T(8,128)} %fusion.39) | copy-start | bytes 12582916
  213.3 14.1 %copy-start.3 = (f32[4,4,512,128]{3,2,1,0:T(8,128)S(1)}, f32[4,4,512,128]{3,2,1,0:T(8,128)}, u32[]{:S(2)}) copy-start(f32[4,4,512,128]{3,2,1,0:T(8,128)} %fusion.15) | copy-start | bytes 12582916
  213.3 14.1 %copy-start.9 = (bf16[512,512]{0,1:T(8,128)(2,1)S(1)}, bf16[512,512]{0,1:T(8,128)(2,1)}, u32[]{:S(2)}) copy-start(bf16[512,512]{0,1:T(8,128)(2,1)} %copy.80) | copy-start | bytes 1572868
  213.4 14.1 %copy-start.17 = (f32[512,4,4]{0,2,1:T(4,128)S(1)}, f32[512,4,4]{0,2,1:T(4,128)}, u32[]{:S(2)}) copy-start(f32[512,4,4]{0,2,1:T(4,128)} %get-tuple-element.20) | copy-start | bytes 98308
  213.4 14.4 %copy-start.21 = (f32[4,4,512,128]{3,2,1,0:T(8,128)S(1)}, f32[4,4,512,128]{3,2,1,0:T(8,128)}, u32[]{:S(2)}) copy-start(f32[4,4,512,128]{3,2,1,0:T(8,128)} %fusion.25) | copy-start | bytes 12582916
  213.4 15.6 %copy-start.22 = (f32[4,4,512,128]{3,2,1,0:T(8,128)S(1)}, f32[4,4,512,128]{3,2,1,0:T(8,128)}, u32[]{:S(2)}) copy-start(f32[4,4,512,128]{3,2,1,0:T(8,128)} %fusion.23) | copy-start | bytes 12582916
  213.4 16.8 %copy-start.23 = (f32[4,4,512,128]{3,2,1,0:T(8,128)S(1)}, f32[4,4,512,128]{3,2,1,0:T(8,128)}, u32[]{:S(2)}) copy-start(f32[4,4,512,128]{3,2,1,0:T(8,128)} %fusion.21) | copy-start | bytes 12582916
where the time goes:
time: 290 us; the launch traced here: 284 us
  matrix products  110 us (38%)
  local copies, waits for them, and re-layouts  45.9 us (16%)
  other arithmetic  38.4 us (13%)
  waiting for transfers between devices  31.2 us (11%)
  starting transfers between devices  29.7 us (10%)
  blocking collectives  28.6 us (10%)
    dot_general x6, matrix products, absorb(): jnp.einsum('kgts,skd->kgtd', weights.astype(jnp.bfloat16), value_heads, p...  66.1 us
    dot_general x6, matrix products, absorb(): jnp.einsum('tkgd,skd->kgts', query_heads, key_heads, preferred_element_ty...  42 us
    reduce_sum x4, other arithmetic, absorb(): running_sum = running_sum * rescale + jnp.sum(weights, axis=-1)  36.8 us
    all_to_all x1, blocking collectives, on_device(): lax.all_to_all(result, 'head', split_axis=0, concat_axis=1, tiled=True)  28.6 us
    ppermute x16, waiting for transfers between devices, partner_2(): lax.ppermute(value, axis, [(i, i ^ 1 << stride) for i in range(lax.axis_s...  24.5 us
    ppermute x16, starting transfers between devices, partner_2(): lax.ppermute(value, axis, [(i, i ^ 1 << stride) for i in range(lax.axis_s...  18.2 us
    ppermute x8, local copies, waits for them, and re-layouts, partner_2(): lax.ppermute(value, axis, [(i, i ^ 1 << stride) for i in range(lax.axis_s...  15.7 us
    unnamed x50, local copies, waits for them, and re-layouts  8.21 us
  transfers between devices with their start and end apart: 19, of which 8 were waited for; matrix products, arithmetic and copies ran while one was open for 10% of the time, Pallas kernels for 0%

commit v1 on v0

v1 whole, which is shorter than its diff:
```python
import functools

import jax
import jax.numpy as jnp
from jax import lax
from jax.experimental import pallas as pl
from jax.experimental.pallas import tpu as pltpu
from jax.sharding import PartitionSpec as P

HD = 128

LOG2E = 1.4426950408889634

def attend(query, key_parts, value_parts, biases, scale):
    scores = [
        lax.dot_general(query, k, (((1,), (1,)), ((), ())), preferred_element_type=jnp.float32)
        for k in key_parts
    ]
    row_max = None
    for s, b in zip(scores, biases):
        top = jnp.max(s, axis=1, keepdims=True) * scale + b
        row_max = top if row_max is None else jnp.maximum(row_max, top)
    total = None
    acc = None
    for s, v, b in zip(scores, value_parts, biases):
        p = jnp.exp2(s * scale + (b - row_max))
        part = jnp.sum(p, axis=1, keepdims=True)
        out = jnp.dot(p.astype(jnp.bfloat16), v, preferred_element_type=jnp.float32)
        total = part if total is None else total + part
        acc = out if acc is None else acc + out
    return acc / total

def kernel(levels, group, head_dim, tile, unroll, bias_ref, q_ref, ko, vo, *rest):
    kp = rest[:levels]; vp = rest[levels:2*levels]; ka, va, o_ref = rest[2*levels:]
    j = pl.program_id(0)
    scale = head_dim ** -0.5 * LOG2E
    ks = [ko] + list(kp) + [ka]; vs = [vo] + list(vp) + [va]
    rows = q_ref.shape[0]
    def step(i, _):
      for u in range(unroll):
        r = pl.multiple_of((i * unroll + u) * tile, tile)
        for g in range(group):
            q = q_ref[pl.ds(r, tile), g*head_dim:(g+1)*head_dim]
            bs = [bias_ref[j*group+g, n] for n in range(levels+2)]
            o = attend(q, [k[...] for k in ks], [v[...] for v in vs], bs, scale)
            o_ref[pl.ds(r, tile), g*head_dim:(g+1)*head_dim] = o.astype(o_ref.dtype)
      return 0
    lax.fori_loop(0, rows // (tile*unroll), step, 0)

def flash(q, ko, vo, kps, vps, ka, va, bias, kv_local, group, head_dim, tile, unroll):
    T = q.shape[0]
    levels = len(kps)
    col = lambda r, w: pl.BlockSpec((r, w), lambda j: (0, j))
    A = ka.shape[0]
    return pl.pallas_call(
        functools.partial(kernel, levels, group, head_dim, tile, unroll),
        grid=(kv_local,),
        in_specs=[pl.BlockSpec(memory_space=pltpu.SMEM), col(T, group*head_dim)] + [col(T, head_dim)]*(2+2*levels) + [col(A, head_dim)]*2,
        out_specs=col(T, group*head_dim),
        out_shape=jax.ShapeDtypeStruct(q.shape, q.dtype),
        name="attend",
    )(bias, q, ko, vo, *kps, *vps, ka, va)


def partner_2(value, axis, stride):
    return lax.ppermute(value, axis, [(i, i ^ 1 << stride) for i in range(lax.axis_size(axis))])


def on_device(queries, keys, values, level_bias, anchor_bias, partners, anchor_positions):
    key_rows = lax.all_to_all(keys, "head", split_axis=1, concat_axis=0, tiled=True)
    value_rows = lax.all_to_all(values, "head", split_axis=1, concat_axis=0, tiled=True)
    query_rows = lax.all_to_all(queries, "head", split_axis=1, concat_axis=0, tiled=True)
    block_rows = query_rows.shape[0]
    kv_local = key_rows.shape[1] // HD
    group_size = level_bias.shape[0] // kv_local
    block_index = lax.axis_index("seq")
    level_count = lax.axis_size("seq").bit_length() - 1
    token_index = block_index * block_rows + jnp.arange(block_rows, dtype=jnp.int32)
    selector = (anchor_positions[:, None] == token_index[None, :]).astype(jnp.bfloat16)
    carried_keys = jnp.dot(selector, key_rows, preferred_element_type=jnp.float32).astype(jnp.bfloat16)
    carried_vals = jnp.dot(selector, value_rows, preferred_element_type=jnp.float32).astype(jnp.bfloat16)
    key_parts, value_parts, biases = [], [], [jnp.zeros_like(anchor_bias)]
    for bit_level in range(level_count):
        pk, pv = partner_2((key_rows, value_rows), "seq", bit_level)
        more_keys, more_vals = partner_2((carried_keys, carried_vals), "seq", bit_level)
        carried_keys = carried_keys + more_keys
        carried_vals = carried_vals + more_vals
        partner = jnp.bitwise_xor(block_index, 1 << bit_level)
        chosen = (partners[0] == partner).astype(jnp.float32)
        key_parts.append(pk)
        value_parts.append(pv)
        biases.append(jnp.sum(level_bias * chosen[None, :], axis=1))
    biases.append(anchor_bias)
    bias = jnp.stack(biases, axis=1) * LOG2E
    tile = min(256, block_rows)
    result = flash(query_rows, key_rows, value_rows, key_parts, value_parts,
                   carried_keys, carried_vals, bias, kv_local, group_size, HD, tile, 1)
    return lax.all_to_all(result, "head", split_axis=0, concat_axis=1, tiled=True)


def solution(mesh):
    in_specs = (
        P(("seq", "head"), None),
        P(("seq", "head"), None),
        P(("seq", "head"), None),
        P("head", None),
        P("head"),
        P("seq", None),
        P(),
    )
    out_specs = P(("seq", "head"), None)
    return jax.shard_map(
        on_device, mesh=mesh, in_specs=in_specs, out_specs=out_specs, check_vma=False
    )
```

time: 290 us -> 165 us (0.57); the launches traced: 284 us -> 165 us
  matrix products: 110 us -> 0.48 us
  Pallas kernels: 0 us -> 38.3 us
  local copies, waits for them, and re-layouts: 45.9 us -> 7.85 us
  other arithmetic: 38.4 us -> 2.08 us
  waiting for transfers between devices: 31.2 us -> 50.5 us
  starting transfers between devices: 29.7 us -> 36.4 us
    dot_general x12 -> x0, matrix products: 108 us -> none  [the longest x6 66.1 us: absorb(): jnp.einsum('kgts,skd->kgtd', weights.astype(jnp.bfloat16), value_heads, p...]
    pallas_call x0 -> x1, Pallas kernels: none -> 38.3 us  [flash(): pl.pallas_call(functools.partial(kernel, levels, group, head_dim, tile, u...]
    reduce_sum x5 -> x1, other arithmetic: 36.9 us -> 0.09 us  [on_device(): biases.append(jnp.sum(level_bias * chosen[None, :], axis=1))]
    ppermute x16, waiting for transfers between devices: 24.5 us -> 40.3 us  [partner_2(): lax.ppermute(value, axis, [(i, i ^ 1 << stride) for i in range(lax.axis_s...]
    ppermute x8 -> x0, local copies, waits for them, and re-layouts: 15.7 us -> none  [partner_2(): lax.ppermute(value, axis, [(i, i ^ 1 << stride) for i in range(lax.axis_s...]
    unnamed x50 -> x18, local copies, waits for them, and re-layouts: 8.21 us -> 1.35 us
    ppermute x16, starting transfers between devices: 18.2 us -> 24.8 us  [partner_2(): lax.ppermute(value, axis, [(i, i ^ 1 << stride) for i in range(lax.axis_s...]
    reshape x5 -> x0, local copies, waits for them, and re-layouts: 5.39 us -> none  [the longest x1 3.49 us: on_device(): query_heads = query_rows.reshape(block_rows, kv_local, group_size, head_dim)]
  transfers between devices with their start and end apart: 19 -> 19, of which waited for: 8 -> 9; matrix products, arithmetic and copies ran while one was open for 10% -> 3% of each run, Pallas kernels for 0% -> 0%
where the time goes in v1:
time: 165 us
  waiting for transfers between devices  50.5 us (31%)
  Pallas kernels  38.3 us (23%)
  starting transfers between devices  36.4 us (22%)
  blocking collectives  28.7 us (17%)
  local copies, waits for them, and re-layouts  7.85 us (5%)
  other arithmetic  2.08 us (1%)
    ppermute x16, waiting for transfers between devices, partner_2(): lax.ppermute(value, axis, [(i, i ^ 1 << stride) for i in range(lax.axis_s...  40.3 us
    pallas_call x1, Pallas kernels, flash(): pl.pallas_call(functools.partial(kernel, levels, group, head_dim, tile, u...  38.3 us
    all_to_all x1, blocking collectives, on_device(): lax.all_to_all(result, 'head', split_axis=0, concat_axis=1, tiled=True)  28.7 us
    ppermute x16, starting transfers between devices, partner_2(): lax.ppermute(value, axis, [(i, i ^ 1 << stride) for i in range(lax.axis_s...  24.8 us
    all_to_all x1, waiting for transfers between devices, on_device(): lax.all_to_all(keys, 'head', split_axis=1, concat_axis=0, tiled=True)  7.88 us
    all_to_all x1, starting transfers between devices, on_device(): lax.all_to_all(keys, 'head', split_axis=1, concat_axis=0, tiled=True)  4.23 us
    all_to_all x1, starting transfers between devices, on_device(): lax.all_to_all(queries, 'head', split_axis=1, concat_axis=0, tiled=True)  3.91 us
    all_to_all x1, starting transfers between devices, on_device(): lax.all_to_all(values, 'head', split_axis=1, concat_axis=0, tiled=True)  3.49 us
  transfers between devices with their start and end apart: 19, of which 9 were waited for; matrix products, arithmetic and copies ran while one was open for 3% of the time, Pallas kernels for 0%

profile of v1, /device:TPU:0, one launch (start us, length us, event | category | flops | bytes accessed | tf_op | source)
XLA Modules:
  0.0 164.5 jit_solution(9259007564273521346)
XLA Ops:
  0.0 2.0 %copy.26 = bf16[32,2,8,512]{3,2,0,1:T(8,128)(2,1)} copy(bf16[32,2,8,512]{3,2,1,0:T(8,128)(2,1)} %bitcast.57) | data formatting | bytes 1048576 | tf_op jit(solution)/shard_map/all_to_all | solution.py:70
  2.0 4.2 %all-to-all-start.1 = ((bf16[256,2,512]{2,0,1:T(8,128)(2,1)}), bf16[256,2,512]{2,0,1:T(8,128)(2,1)S(1)}, u32[]{:S(2)}, u32[]{:S(2)}) async-start(bf16[256,2,512]{2,0,1:T(8,128)(2,1)} %bitcast.39), calls=%async_computation.1 | async-start | bytes 1048576 | tf_op jit(solution)/shard_map/all_to_all | solution.py:70
  6.3 0.0 copy-done.4
  6.3 0.8 copy.25
  7.1 7.9 %all-to-all-done.1 = bf16[256,2,512]{2,0,1:T(8,128)(2,1)S(1)} async-done(((bf16[256,2,512]{2,0,1:T(8,128)(2,1)}), bf16[256,2,512]{2,0,1:T(8,128)(2,1)S(1)}, u32[]{:S(2)}, u32[]{:S(2)}) %all-to-all-start.1) | async-done | bytes 524320 | tf_op jit(solution)/shard_map/all_to_all | solution.py:70
  15.0 3.5 %all-to-all-start.2 = ((bf16[256,2,512]{2,0,1:T(8,128)(2,1)}), bf16[256,2,512]{2,0,1:T(8,128)(2,1)S(1)}, u32[]{:S(2)}, u32[]{:S(2)}) async-start(bf16[256,2,512]{2,0,1:T(8,128)(2,1)} %bitcast.56), calls=%async_computation.2 | async-start | bytes 1048576 | tf_op jit(solution)/shard_map/all_to_all | solution.py:71
  18.5 0.0 copy-done.3
  18.5 0.0 copy-start.6
  18.5 1.6 copy.24
  20.1 0.0 collective-permute-start
  20.1 1.8 %collective-permute-start.1 = (bf16[512,512]{1,0:T(8,128)(2,1)S(1)}, bf16[512,512]{1,0:T(8,128)(2,1)}, u32[]{:S(2)}, u32[]{:S(2)}) collective-permute-start(bf16[512,512]{1,0:T(8,128)(2,1)S(1)} %bitcast.44), channel_id=1, source_target_pairs={{0,4},{2,6},{4,0},{6,2},{8,12},{10,14},{12,8},{14,10},{16,20},{18,... | collective-permute-start | bytes 1572872 | tf_op jit(solution)/shard_map/ppermute | solution.py:66
  21.9 1.6 collective-permute-start.2
  23.4 0.0 copy-done.6
  23.4 0.2 convolution_convert_fusion.1
  23.7 0.1 collective-permute-start.8
  23.8 2.4 %all-to-all-done.2 = bf16[256,2,512]{2,0,1:T(8,128)(2,1)S(1)} async-done(((bf16[256,2,512]{2,0,1:T(8,128)(2,1)}), bf16[256,2,512]{2,0,1:T(8,128)(2,1)S(1)}, u32[]{:S(2)}, u32[]{:S(2)}) %all-to-all-start.2) | async-done | bytes 524320 | tf_op jit(solution)/shard_map/all_to_all | solution.py:71
  26.2 3.9 %all-to-all-start = ((bf16[256,2,2048]{2,0,1:T(8,128)(2,1)}), bf16[256,2,2048]{2,0,1:T(8,128)(2,1)S(1)}, u32[]{:S(2)}, u32[]{:S(2)}) async-start(bf16[256,2,2048]{2,0,1:T(8,128)(2,1)} %bitcast.37), calls=%async_computation | async-start | bytes 4194304 | tf_op jit(solution)/shard_map/all_to_all | solution.py:72
  30.1 0.2 convolution_convert_fusion
  30.3 0.1 collective-permute-start.12
  30.4 0.0 collective-permute-done.8
  30.4 1.6 collective-permute-start.9
  32.0 0.0 collective-permute-done.12
  32.0 1.2 collective-permute-start.13
  33.2 3.1 %collective-permute-done.9 = bf16[64,512]{1,0:T(8,128)(2,1)S(1)} collective-permute-done((bf16[64,512]{1,0:T(8,128)(2,1)S(1)}, bf16[64,512]{1,0:T(8,128)(2,1)S(1)}, u32[]{:S(2)}, u32[]{:S(2)}) %collective-permute-start.9) | collective-permute-done | bytes 65568 | tf_op jit(solution)/shard_map/ppermute | solution.py:66
  36.3 1.9 %collective-permute-start.10 = (bf16[64,512]{1,0:T(8,128)(2,1)S(1)}, bf16[64,512]{1,0:T(8,128)(2,1)S(1)}, u32[]{:S(2)}, u32[]{:S(2)}) collective-permute-start(bf16[64,512]{1,0:T(8,128)(2,1)S(1)} %add.37), channel_id=1, source_target_pairs={{0,8},{2,10},{4,12},{6,14},{8,0},{10,2},{12,4},{14,6},{16,24},{18,... | collective-permute-start | bytes 196616 | tf_op jit(solution)/shard_map/ppermute | solution.py:66
  38.2 0.0 collective-permute-done.13
  38.2 0.9 collective-permute-start.14
  39.2 2.2 %collective-permute-done.10 = bf16[64,512]{1,0:T(8,128)(2,1)S(1)} collective-permute-done((bf16[64,512]{1,0:T(8,128)(2,1)S(1)}, bf16[64,512]{1,0:T(8,128)(2,1)S(1)}, u32[]{:S(2)}, u32[]{:S(2)}) %collective-permute-start.10) | collective-permute-done | bytes 65568 | tf_op jit(solution)/shard_map/ppermute | solution.py:66
  41.3 2.7 %collective-permute-start.11 = (bf16[64,512]{1,0:T(8,128)(2,1)S(1)}, bf16[64,512]{1,0:T(8,128)(2,1)S(1)}, u32[]{:S(2)}, u32[]{:S(2)}) collective-permute-start(bf16[64,512]{1,0:T(8,128)(2,1)S(1)} %add.38), channel_id=1, source_target_pairs={{0,16},{2,18},{4,20},{6,22},{8,24},{10,26},{12,28},{14,30},{16,0},... | collective-permute-start | bytes 196616 | tf_op jit(solution)/shard_map/ppermute | solution.py:66
  44.0 0.0 collective-permute-done.14
  44.0 1.9 %collective-permute-start.15 = (bf16[64,512]{1,0:T(8,128)(2,1)S(1)}, bf16[64,512]{1,0:T(8,128)(2,1)S(1)}, u32[]{:S(2)}, u32[]{:S(2)}) collective-permute-start(bf16[64,512]{1,0:T(8,128)(2,1)S(1)} %add.42), channel_id=1, source_target_pairs={{0,16},{2,18},{4,20},{6,22},{8,24},{10,26},{12,28},{14,30},{16,0},... | collective-permute-start | bytes 196616 | tf_op jit(solution)/shard_map/ppermute | solution.py:66
  45.9 2.5 %collective-permute-done.11 = bf16[64,512]{1,0:T(8,128)(2,1)S(1)} collective-permute-done((bf16[64,512]{1,0:T(8,128)(2,1)S(1)}, bf16[64,512]{1,0:T(8,128)(2,1)S(1)}, u32[]{:S(2)}, u32[]{:S(2)}) %collective-permute-start.11) | collective-permute-done | bytes 65568 | tf_op jit(solution)/shard_map/ppermute | solution.py:66
  48.4 0.0 copy-done.1
  48.4 0.7 collective-permute-start.3
  49.2 7.1 %collective-permute-done.15 = bf16[64,512]{1,0:T(8,128)(2,1)S(1)} collective-permute-done((bf16[64,512]{1,0:T(8,128)(2,1)S(1)}, bf16[64,512]{1,0:T(8,128)(2,1)S(1)}, u32[]{:S(2)}, u32[]{:S(2)}) %collective-permute-start.15) | collective-permute-done | bytes 65568 | tf_op jit(solution)/shard_map/ppermute | solution.py:66
  56.3 0.0 collective-permute-start.4
  56.3 0.0 collective-permute-done.rest_0_
  56.3 1.4 collective-permute-start.5
  57.7 0.0 collective-permute-done.1.rest_1_
  57.7 7.7 %collective-permute-start.6 = (bf16[512,512]{1,0:T(8,128)(2,1)S(1)}, bf16[512,512]{1,0:T(8,128)(2,1)}, u32[]{:S(2)}, u32[]{:S(2)}) collective-permute-start(bf16[512,512]{1,0:T(8,128)(2,1)S(1)} %bitcast.52), channel_id=1, source_target_pairs={{0,8},{2,10},{4,12},{6,14},{8,0},{10,2},{12,4},{14,6},{16,24},{18,... | collective-permute-start | bytes 1572872 | tf_op jit(solution)/shard_map/ppermute | solution.py:66
  65.4 0.0 collective-permute-done.2.rest_2_
  65.4 1.3 collective-permute-start.7
  66.7 0.0 copy-done.5
  66.7 0.1 multiply_reduce_fusion
  66.8 0.1 copy.8
  66.9 0.1 copy.9
  67.0 0.1 copy.10
  67.1 0.1 copy.11
  67.2 0.0 copy-done.8
  67.2 0.1 copy.12
  67.3 0.1 stack.23
  67.3 0.6 broadcast_multiply_fusion.bias_ref
  68.0 0.6 add.39.rest_8_
  68.6 0.6 add.43.rest_9_
  69.2 2.3 %collective-permute-done.3.rest_3_ = bf16[512,512]{1,0:T(8,128)(2,1)} collective-permute-done((bf16[512,512]{1,0:T(8,128)(2,1)S(1)}, bf16[512,512]{1,0:T(8,128)(2,1)}, u32[]{:S(2)}, u32[]{:S(2)}) %collective-permute-start.3) | collective-permute-done | bytes 524320 | tf_op jit(solution)/shard_map/ppermute | solution.py:66
  71.6 0.0 collective-permute-done.4.rest_4_
  71.6 0.0 collective-permute-done.5.rest_5_
  71.6 17.4 %collective-permute-done.6.rest_6_ = bf16[512,512]{1,0:T(8,128)(2,1)} collective-permute-done((bf16[512,512]{1,0:T(8,128)(2,1)S(1)}, bf16[512,512]{1,0:T(8,128)(2,1)}, u32[]{:S(2)}, u32[]{:S(2)}) %collective-permute-start.6) | collective-permute-done | bytes 524320 | tf_op jit(solution)/shard_map/ppermute | solution.py:66
  89.0 5.6 %collective-permute-done.7.rest_7_ = bf16[512,512]{1,0:T(8,128)(2,1)} collective-permute-done((bf16[512,512]{1,0:T(8,128)(2,1)S(1)}, bf16[512,512]{1,0:T(8,128)(2,1)}, u32[]{:S(2)}, u32[]{:S(2)}) %collective-permute-start.7) | collective-permute-done | bytes 524320 | tf_op jit(solution)/shard_map/ppermute | solution.py:66
  94.6 0.0 all-to-all-done
  94.6 1.3 copy-done
  95.9 38.3 %attend.1 = bf16[512,2048]{1,0:T(8,128)(2,1)} custom-call(f32[16,6]{1,0:T(8,128)} %broadcast_multiply_fusion.bias_ref, bf16[512,2048]{1,0:T(8,128)(2,1)} %bitcast.41, bf16[512,512]{1,0:T(8,128)(2,1)} %bitcast.48, bf16[512,512]{1,0:T(8,128)(2,1)} %bitcast.54, bf16[512,512]{1,0:T(8,128)(2,1)} %collective-permute-done.rest_0_, ...), custom_call_target="tpu_custom_call" | custom-call | tf_op jit(solution)/shard_map/attend/pallas_call | solution.py:55
  134.2 28.7 %all_to_all.76 = bf16[2,256,2048]{2,1,0:T(8,128)(2,1)S(1)} all-to-all(bf16[2,256,2048]{2,1,0:T(8,128)(2,1)} %bitcast.42), channel_id=1, replica_groups=mesh['seq'=16,'head'=2] {'head'}, dimensions={0} | all-to-all | bytes 4194304 | tf_op jit(solution)/shard_map/all_to_all | solution.py:98
  163.0 1.6 copy.20
  (19 shorter events, 0.1 us)
Async XLA Ops:
  0.0 6.3 %copy-start.4 = (bf16[256,1024]{1,0:T(8,128)(2,1)S(1)}, bf16[256,1024]{1,0:T(8,128)(2,1)}, u32[]{:S(2)}) copy-start(bf16[256,1024]{1,0:T(8,128)(2,1)} %param.9) | copy-start | bytes 1572868
  0.0 18.5 %copy-start.3 = (bf16[256,4096]{1,0:T(8,128)(2,1)S(1)}, bf16[256,4096]{1,0:T(8,128)(2,1)}, u32[]{:S(2)}) copy-start(bf16[256,4096]{1,0:T(8,128)(2,1)} %param.7) | copy-start | bytes 6291460
  2.0 13.0 %all-to-all-start.1 = ((bf16[256,2,512]{2,0,1:T(8,128)(2,1)}), bf16[256,2,512]{2,0,1:T(8,128)(2,1)S(1)}, u32[]{:S(2)}, u32[]{:S(2)}) async-start(bf16[256,2,512]{2,0,1:T(8,128)(2,1)} %bitcast.39), calls=%async_computation.1 | async-start | bytes 1048576 | tf_op jit(solution)/shard_map/all_to_all | solution.py:70
  15.0 33.4 %copy-start.1 = (bf16[256,2,512]{2,0,1:T(8,128)(2,1)}, bf16[256,2,512]{2,0,1:T(8,128)(2,1)S(1)}, u32[]{:S(2)}) copy-start(bf16[256,2,512]{2,0,1:T(8,128)(2,1)S(1)} %all-to-all-done.1) | copy-start | bytes 1572868
  15.0 11.2 %all-to-all-start.2 = ((bf16[256,2,512]{2,0,1:T(8,128)(2,1)}), bf16[256,2,512]{2,0,1:T(8,128)(2,1)S(1)}, u32[]{:S(2)}, u32[]{:S(2)}) async-start(bf16[256,2,512]{2,0,1:T(8,128)(2,1)} %bitcast.56), calls=%async_computation.2 | async-start | bytes 1048576 | tf_op jit(solution)/shard_map/all_to_all | solution.py:71
  18.5 4.9 %copy-start.6 = (s32[64]{0:T(128)S(1)}, s32[64]{0:T(128)}, u32[]{:S(2)}) copy-start(s32[64]{0:T(128)} %param.13) | copy-start | bytes 772
  20.1 36.2 %collective-permute-start = (bf16[512,512]{1,0:T(8,128)(2,1)S(1)}, bf16[512,512]{1,0:T(8,128)(2,1)}, u32[]{:S(2)}, u32[]{:S(2)}) collective-permute-start(bf16[512,512]{1,0:T(8,128)(2,1)S(1)} %bitcast.43), channel_id=1, source_target_pairs={{0,2},{2,0},{4,6},{6,4},{8,10},{10,8},{12,14},{14,12},{16,18},{18,... | collective-permute-start | bytes 1572872 | tf_op jit(solution)/shard_map/ppermute | solution.py:66
  20.1 37.6 %collective-permute-start.1 = (bf16[512,512]{1,0:T(8,128)(2,1)S(1)}, bf16[512,512]{1,0:T(8,128)(2,1)}, u32[]{:S(2)}, u32[]{:S(2)}) collective-permute-start(bf16[512,512]{1,0:T(8,128)(2,1)S(1)} %bitcast.44), channel_id=1, source_target_pairs={{0,4},{2,6},{4,0},{6,2},{8,12},{10,14},{12,8},{14,10},{16,20},{18,... | collective-permute-start | bytes 1572872 | tf_op jit(solution)/shard_map/ppermute | solution.py:66
  21.9 43.5 %collective-permute-start.2 = (bf16[512,512]{1,0:T(8,128)(2,1)S(1)}, bf16[512,512]{1,0:T(8,128)(2,1)}, u32[]{:S(2)}, u32[]{:S(2)}) collective-permute-start(bf16[512,512]{1,0:T(8,128)(2,1)S(1)} %bitcast.45), channel_id=1, source_target_pairs={{0,8},{2,10},{4,12},{6,14},{8,0},{10,2},{12,4},{14,6},{16,24},{18,... | collective-permute-start | bytes 1572872 | tf_op jit(solution)/shard_map/ppermute | solution.py:66
  23.7 6.7 %collective-permute-start.8 = (bf16[64,512]{1,0:T(8,128)(2,1)S(1)}, bf16[64,512]{1,0:T(8,128)(2,1)S(1)}, u32[]{:S(2)}, u32[]{:S(2)}) collective-permute-start(bf16[64,512]{1,0:T(8,128)(2,1)S(1)} %convolution_convert_fusion.1), channel_id=1, source_target_pairs={{0,2},{2,0},{4,6},{6,4},{8,10},{10,8},{12,14},{14,12},{16,18},{18,... | collective-permute-start | bytes 196616 | tf_op jit(solution)/shard_map/ppermute | solution.py:66
  26.1 39.3 %copy-start.2 = (bf16[256,2,512]{2,0,1:T(8,128)(2,1)}, bf16[256,2,512]{2,0,1:T(8,128)(2,1)S(1)}, u32[]{:S(2)}) copy-start(bf16[256,2,512]{2,0,1:T(8,128)(2,1)S(1)} %all-to-all-done.2) | copy-start | bytes 1572868
  26.2 40.6 %copy-start.7 = (s32[1,4]{1,0:T(1,128)S(1)}, s32[1,4]{1,0:T(1,128)}, u32[]{:S(2)}) copy-start(s32[1,4]{1,0:T(1,128)} %param.12) | copy-start | bytes 52
  26.2 40.6 %copy-start.5 = (f32[16,4]{0,1:T(4,128)S(1)}, f32[16,4]{0,1:T(4,128)}, u32[]{:S(2)}) copy-start(f32[16,4]{0,1:T(4,128)} %param.10) | copy-start | bytes 772
  26.2 41.0 %copy-start.8 = (f32[16]{0:T(128)S(1)}, f32[16]{0:T(128)}, u32[]{:S(2)}) copy-start(f32[16]{0:T(128)} %param.11) | copy-start | bytes 196
  26.2 68.5 %all-to-all-start = ((bf16[256,2,2048]{2,0,1:T(8,128)(2,1)}), bf16[256,2,2048]{2,0,1:T(8,128)(2,1)S(1)}, u32[]{:S(2)}, u32[]{:S(2)}) async-start(bf16[256,2,2048]{2,0,1:T(8,128)(2,1)} %bitcast.37), calls=%async_computation | async-start | bytes 4194304 | tf_op jit(solution)/shard_map/all_to_all | solution.py:72
  30.3 1.7 %collective-permute-start.12 = (bf16[64,512]{1,0:T(8,128)(2,1)S(1)}, bf16[64,512]{1,0:T(8,128)(2,1)S(1)}, u32[]{:S(2)}, u32[]{:S(2)}) collective-permute-start(bf16[64,512]{1,0:T(8,128)(2,1)S(1)} %convolution_convert_fusion), channel_id=1, source_target_pairs={{0,2},{2,0},{4,6},{6,4},{8,10},{10,8},{12,14},{14,12},{16,18},{18,... | collective-permute-start | bytes 196616 | tf_op jit(solution)/shard_map/ppermute | solution.py:66
  30.4 5.8 %collective-permute-start.9 = (bf16[64,512]{1,0:T(8,128)(2,1)S(1)}, bf16[64,512]{1,0:T(8,128)(2,1)S(1)}, u32[]{:S(2)}, u32[]{:S(2)}) collective-permute-start(bf16[64,512]{1,0:T(8,128)(2,1)S(1)} %add.36), channel_id=1, source_target_pairs={{0,4},{2,6},{4,0},{6,2},{8,12},{10,14},{12,8},{14,10},{16,20},{18,... | collective-permute-start | bytes 196616 | tf_op jit(solution)/shard_map/ppermute | solution.py:66
  32.0 6.2 %collective-permute-start.13 = (bf16[64,512]{1,0:T(8,128)(2,1)S(1)}, bf16[64,512]{1,0:T(8,128)(2,1)S(1)}, u32[]{:S(2)}, u32[]{:S(2)}) collective-permute-start(bf16[64,512]{1,0:T(8,128)(2,1)S(1)} %add.40), channel_id=1, source_target_pairs={{0,4},{2,6},{4,0},{6,2},{8,12},{10,14},{12,8},{14,10},{16,20},{18,... | collective-permute-start | bytes 196616 | tf_op jit(solution)/shard_map/ppermute | solution.py:66
  36.3 5.0 %collective-permute-start.10 = (bf16[64,512]{1,0:T(8,128)(2,1)S(1)}, bf16[64,512]{1,0:T(8,128)(2,1)S(1)}, u32[]{:S(2)}, u32[]{:S(2)}) collective-permute-start(bf16[64,512]{1,0:T(8,128)(2,1)S(1)} %add.37), channel_id=1, source_target_pairs={{0,8},{2,10},{4,12},{6,14},{8,0},{10,2},{12,4},{14,6},{16,24},{18,... | collective-permute-start | bytes 196616 | tf_op jit(solution)/shard_map/ppermute | solution.py:66
  38.2 5.8 %collective-permute-start.14 = (bf16[64,512]{1,0:T(8,128)(2,1)S(1)}, bf16[64,512]{1,0:T(8,128)(2,1)S(1)}, u32[]{:S(2)}, u32[]{:S(2)}) collective-permute-start(bf16[64,512]{1,0:T(8,128)(2,1)S(1)} %add.41), channel_id=1, source_target_pairs={{0,8},{2,10},{4,12},{6,14},{8,0},{10,2},{12,4},{14,6},{16,24},{18,... | collective-permute-start | bytes 196616 | tf_op jit(solution)/shard_map/ppermute | solution.py:66
  41.3 7.1 %collective-permute-start.11 = (bf16[64,512]{1,0:T(8,128)(2,1)S(1)}, bf16[64,512]{1,0:T(8,128)(2,1)S(1)}, u32[]{:S(2)}, u32[]{:S(2)}) collective-permute-start(bf16[64,512]{1,0:T(8,128)(2,1)S(1)} %add.38), channel_id=1, source_target_pairs={{0,16},{2,18},{4,20},{6,22},{8,24},{10,26},{12,28},{14,30},{16,0},... | collective-permute-start | bytes 196616 | tf_op jit(solution)/shard_map/ppermute | solution.py:66
  44.0 12.2 %collective-permute-start.15 = (bf16[64,512]{1,0:T(8,128)(2,1)S(1)}, bf16[64,512]{1,0:T(8,128)(2,1)S(1)}, u32[]{:S(2)}, u32[]{:S(2)}) collective-permute-start(bf16[64,512]{1,0:T(8,128)(2,1)S(1)} %add.42), channel_id=1, source_target_pairs={{0,16},{2,18},{4,20},{6,22},{8,24},{10,26},{12,28},{14,30},{16,0},... | collective-permute-start | bytes 196616 | tf_op jit(solution)/shard_map/ppermute | solution.py:66
  48.4 23.1 %collective-permute-start.3 = (bf16[512,512]{1,0:T(8,128)(2,1)S(1)}, bf16[512,512]{1,0:T(8,128)(2,1)}, u32[]{:S(2)}, u32[]{:S(2)}) collective-permute-start(bf16[512,512]{1,0:T(8,128)(2,1)S(1)} %bitcast.47), channel_id=1, source_target_pairs={{0,16},{2,18},{4,20},{6,22},{8,24},{10,26},{12,28},{14,30},{16,0},... | collective-permute-start | bytes 1572872 | tf_op jit(solution)/shard_map/ppermute | solution.py:66
  56.3 15.3 %collective-permute-start.4 = (bf16[512,512]{1,0:T(8,128)(2,1)S(1)}, bf16[512,512]{1,0:T(8,128)(2,1)}, u32[]{:S(2)}, u32[]{:S(2)}) collective-permute-start(bf16[512,512]{1,0:T(8,128)(2,1)S(1)} %bitcast.50), channel_id=1, source_target_pairs={{0,2},{2,0},{4,6},{6,4},{8,10},{10,8},{12,14},{14,12},{16,18},{18,... | collective-permute-start | bytes 1572872 | tf_op jit(solution)/shard_map/ppermute | solution.py:66
  56.3 15.3 %collective-permute-start.5 = (bf16[512,512]{1,0:T(8,128)(2,1)S(1)}, bf16[512,512]{1,0:T(8,128)(2,1)}, u32[]{:S(2)}, u32[]{:S(2)}) collective-permute-start(bf16[512,512]{1,0:T(8,128)(2,1)S(1)} %bitcast.51), channel_id=1, source_target_pairs={{0,4},{2,6},{4,0},{6,2},{8,12},{10,14},{12,8},{14,10},{16,20},{18,... | collective-permute-start | bytes 1572872 | tf_op jit(solution)/shard_map/ppermute | solution.py:66
  57.7 31.3 %collective-permute-start.6 = (bf16[512,512]{1,0:T(8,128)(2,1)S(1)}, bf16[512,512]{1,0:T(8,128)(2,1)}, u32[]{:S(2)}, u32[]{:S(2)}) collective-permute-start(bf16[512,512]{1,0:T(8,128)(2,1)S(1)} %bitcast.52), channel_id=1, source_target_pairs={{0,8},{2,10},{4,12},{6,14},{8,0},{10,2},{12,4},{14,6},{16,24},{18,... | collective-permute-start | bytes 1572872 | tf_op jit(solution)/shard_map/ppermute | solution.py:66
  65.4 29.2 %collective-permute-start.7 = (bf16[512,512]{1,0:T(8,128)(2,1)S(1)}, bf16[512,512]{1,0:T(8,128)(2,1)}, u32[]{:S(2)}, u32[]{:S(2)}) collective-permute-start(bf16[512,512]{1,0:T(8,128)(2,1)S(1)} %bitcast.53), channel_id=1, source_target_pairs={{0,16},{2,18},{4,20},{6,22},{8,24},{10,26},{12,28},{14,30},{16,0},... | collective-permute-start | bytes 1572872 | tf_op jit(solution)/shard_map/ppermute | solution.py:66
  94.6 1.3 copy-start

commit v2 on v1

v2 whole, which is shorter than its diff:
```python
import functools

import jax
import jax.numpy as jnp
from jax import lax
from jax.experimental import pallas as pl
from jax.experimental.pallas import tpu as pltpu
from jax.sharding import PartitionSpec as P

HD = 128
LOG2E = 1.4426950408889634


def attend(query, key_parts, value_parts, biases, scale):
    scores = [
        lax.dot_general(query, k, (((1,), (1,)), ((), ())), preferred_element_type=jnp.float32)
        for k in key_parts
    ]
    row_max = None
    for s, b in zip(scores, biases):
        top = jnp.max(s, axis=1, keepdims=True) * scale + b
        row_max = top if row_max is None else jnp.maximum(row_max, top)
    total = None
    acc = None
    for s, v, b in zip(scores, value_parts, biases):
        p = jnp.exp2(s * scale + (b - row_max))
        part = jnp.sum(p, axis=1, keepdims=True)
        out = jnp.dot(p.astype(jnp.bfloat16), v, preferred_element_type=jnp.float32)
        total = part if total is None else total + part
        acc = out if acc is None else acc + out
    return acc / total


def kernel(
    heads, levels, kv_local, group,
    bias_ref, sel_ref, keys_ref, values_ref, queries_ref, out_ref,
    blocks, qbuf, obuf, part, part_in, carry, carry_in,
    part_send, part_recv, carry_send, carry_recv,
    own_sem, x_send, x_recv, own_q_sem, q_send, q_recv,
    lv_send, lv_recv, own_o_sem, o_send, o_recv,
):
    me = lax.axis_index("head")
    seat = lax.axis_index("seq")
    t = keys_ref.shape[0]
    wide = group * HD
    scale = HD ** -0.5 * LOG2E
    mesh_id = pl.DeviceIdType.MESH

    def peer(d):
        return lax.rem(me + d, heads)

    def partner(l):
        bit = lax.rem(lax.div(seat, 1 << l), 2)
        return seat + (1 - 2 * bit) * (1 << l)

    barrier = pltpu.get_barrier_semaphore()
    for d in range(1, heads):
        pl.semaphore_signal(barrier, inc=1, device_id={"head": peer(d)}, device_id_type=mesh_id)
    for l in range(levels):
        pl.semaphore_signal(barrier, inc=1, device_id={"seq": partner(l)}, device_id_type=mesh_id)

    def cols(owner, j, width):
        return pl.ds(pl.multiple_of((owner * kv_local + j) * width, width), width)

    def rows(owner):
        return pl.ds(pl.multiple_of(owner * t, t), t)

    def own_copy(j, c):
        src = (keys_ref, values_ref)[c]
        return pltpu.make_async_copy(
            src.at[:, cols(me, j, HD)], blocks.at[0, j, c, rows(me)], own_sem.at[j, c])

    def own_q(j):
        return pltpu.make_async_copy(
            queries_ref.at[:, cols(me, j, wide)], qbuf.at[j, rows(me)], own_q_sem.at[j])

    def send_kv(j, c, d):
        src = (keys_ref, values_ref)[c]
        return pltpu.make_async_remote_copy(
            src_ref=src.at[:, cols(peer(d), j, HD)], dst_ref=blocks.at[0, j, c, rows(me)],
            send_sem=x_send.at[j, c, d], recv_sem=x_recv.at[j, c, d],
            device_id={"head": peer(d)}, device_id_type=mesh_id)

    def came_kv(j, c, d):
        src = (keys_ref, values_ref)[c]
        return pltpu.make_async_remote_copy(
            src_ref=src.at[:, cols(me, j, HD)], dst_ref=blocks.at[0, j, c, rows(peer(heads - d))],
            send_sem=x_send.at[j, c, d], recv_sem=x_recv.at[j, c, d],
            device_id={"head": peer(d)}, device_id_type=mesh_id)

    def send_q(j, d):
        return pltpu.make_async_remote_copy(
            src_ref=queries_ref.at[:, cols(peer(d), j, wide)], dst_ref=qbuf.at[j, rows(me)],
            send_sem=q_send.at[j, d], recv_sem=q_recv.at[j, d],
            device_id={"head": peer(d)}, device_id_type=mesh_id)

    def came_q(j, d):
        return pltpu.make_async_remote_copy(
            src_ref=queries_ref.at[:, cols(me, j, wide)], dst_ref=qbuf.at[j, rows(peer(heads - d))],
            send_sem=q_send.at[j, d], recv_sem=q_recv.at[j, d],
            device_id={"head": peer(d)}, device_id_type=mesh_id)

    def send_level(j, l):
        return pltpu.make_async_remote_copy(
            src_ref=blocks.at[0, j], dst_ref=blocks.at[l + 1, j],
            send_sem=lv_send.at[j, l], recv_sem=lv_recv.at[j, l],
            device_id={"seq": partner(l)}, device_id_type=mesh_id)

    def send_part(d):
        return pltpu.make_async_remote_copy(
            src_ref=part.at[d], dst_ref=part_in.at[d],
            send_sem=part_send.at[d], recv_sem=part_recv.at[d],
            device_id={"head": peer(d)}, device_id_type=mesh_id)

    def send_carry(l):
        return pltpu.make_async_remote_copy(
            src_ref=carry.at[l + 1], dst_ref=carry_in.at[l],
            send_sem=carry_send.at[l], recv_sem=carry_recv.at[l],
            device_id={"seq": partner(l)}, device_id_type=mesh_id)

    def send_out(j, d):
        return pltpu.make_async_remote_copy(
            src_ref=obuf.at[j, d], dst_ref=out_ref.at[:, cols(me, j, wide)],
            send_sem=o_send.at[j, d], recv_sem=o_recv.at[j, d],
            device_id={"head": peer(d)}, device_id_type=mesh_id)

    def came_out(j, d):
        return pltpu.make_async_remote_copy(
            src_ref=obuf.at[j, d], dst_ref=out_ref.at[:, cols(peer(heads - d), j, wide)],
            send_sem=o_send.at[j, d], recv_sem=o_recv.at[j, d],
            device_id={"head": peer(d)}, device_id_type=mesh_id)

    def own_out(j):
        return pltpu.make_async_copy(
            obuf.at[j, 0], out_ref.at[:, cols(me, j, wide)], own_o_sem.at[j])

    for j in range(kv_local):
        for c in range(2):
            own_copy(j, c).start()
        own_q(j).start()
    for d in range(heads):
        for j in range(kv_local):
            for c in range(2):
                src = (keys_ref, values_ref)[c]
                part[d, j, c] = jnp.dot(
                    sel_ref[...], src[:, cols(peer(d), j, HD)], preferred_element_type=jnp.float32
                ).astype(jnp.bfloat16)
    pl.semaphore_wait(barrier, heads - 1 + levels)
    for d in range(1, heads):
        send_part(d).start()
    for j in range(kv_local):
        for d in range(1, heads):
            for c in range(2):
                send_kv(j, c, d).start()
    for j in range(kv_local):
        for d in range(1, heads):
            send_q(j, d).start()

    def forward(j):
        for c in range(2):
            own_copy(j, c).wait()
            for d in range(1, heads):
                came_kv(j, c, d).wait_recv()
        for l in reversed(range(levels)):
            send_level(j, l).start()

    held = part[0].astype(jnp.float32)
    for d in range(1, heads):
        send_part(d).wait_recv()
        held = held + part_in[d].astype(jnp.float32)
    carry[levels] = held.astype(jnp.bfloat16)
    sent = 0
    for l in reversed(range(levels)):
        send_carry(l).start()
        if sent < kv_local:
            forward(sent)
            sent += 1
        send_carry(l).wait_recv()
        carry[l] = (carry[l + 1].astype(jnp.float32) + carry_in[l].astype(jnp.float32)).astype(
            jnp.bfloat16)
    for j in range(sent, kv_local):
        forward(j)

    def one(step, _):
        j = lax.div(step, heads)
        turn = lax.rem(step, heads)

        @pl.when(turn == 0)
        def _():
            own_q(j).wait()
            for d in range(1, heads):
                came_q(j, d).wait_recv()
            for l in range(levels):
                send_level(j, l).wait_recv()

        d = lax.rem(turn + 1, heads)
        here = rows(peer(d))
        for g in range(group):
            result = attend(
                qbuf[j, here, g * HD:(g + 1) * HD],
                [blocks[n, j, 0] for n in range(levels + 1)] + [carry[0, j, 0]],
                [blocks[n, j, 1] for n in range(levels + 1)] + [carry[0, j, 1]],
                [bias_ref[j * group + g, n] for n in range(levels + 2)],
                scale,
            )
            obuf[j, d, :, g * HD:(g + 1) * HD] = result.astype(jnp.bfloat16)

        @pl.when(turn < heads - 1)
        def _():
            send_out(j, d).start()

        @pl.when(turn == heads - 1)
        def _():
            own_out(j).start()

        return 0

    lax.fori_loop(0, kv_local * heads, one, 0)

    for d in range(1, heads):
        send_part(d).wait_send()
    for l in range(levels):
        send_carry(l).wait_send()
    for j in range(kv_local):
        own_out(j).wait()
        for l in range(levels):
            send_level(j, l).wait_send()
        for d in range(1, heads):
            for c in range(2):
                send_kv(j, c, d).wait_send()
            send_q(j, d).wait_send()
            send_out(j, d).wait_send()
            came_out(j, d).wait_recv()


def on_device(queries, keys, values, level_bias, anchor_bias, partners, anchor_positions):
    t = queries.shape[0]
    heads = lax.axis_size("head")
    levels = lax.axis_size("seq").bit_length() - 1
    kv_local = keys.shape[1] // HD // heads
    group = level_bias.shape[0] // kv_local
    anchors = anchor_positions.shape[0]
    block_index = lax.axis_index("seq")
    first = (block_index * heads + lax.axis_index("head")) * t
    token_index = first + jnp.arange(t, dtype=jnp.int32)
    selector = (anchor_positions[:, None] == token_index[None, :]).astype(jnp.bfloat16)
    biases = [jnp.zeros_like(anchor_bias)]
    for l in range(levels):
        chosen = (partners[0] == jnp.bitwise_xor(block_index, 1 << l)).astype(jnp.float32)
        biases.append(jnp.sum(level_bias * chosen[None, :], axis=1))
    biases.append(anchor_bias)
    bias = jnp.stack(biases, axis=1) * LOG2E
    vmem = pl.BlockSpec(memory_space=pltpu.VMEM)
    dma = pltpu.SemaphoreType.DMA
    anchor_shape = (kv_local, 2, anchors, HD)
    bf16 = jnp.bfloat16
    return pl.pallas_call(
        functools.partial(kernel, heads, levels, kv_local, group),
        in_specs=[pl.BlockSpec(memory_space=pltpu.SMEM), vmem, vmem, vmem,
                  pl.BlockSpec(memory_space=pl.ANY)],
        out_specs=pl.BlockSpec(memory_space=pl.ANY),
        out_shape=jax.ShapeDtypeStruct(queries.shape, queries.dtype),
        scratch_shapes=[
            pltpu.VMEM((levels + 1, kv_local, 2, t * heads, HD), bf16),
            pltpu.VMEM((kv_local, t * heads, group * HD), bf16),
            pltpu.VMEM((kv_local, heads, t, group * HD), bf16),
            pltpu.VMEM((heads,) + anchor_shape, bf16),
            pltpu.VMEM((heads,) + anchor_shape, bf16),
            pltpu.VMEM((levels + 1,) + anchor_shape, bf16),
            pltpu.VMEM((levels,) + anchor_shape, bf16),
            dma((heads,)), dma((heads,)), dma((levels,)), dma((levels,)),
            dma((kv_local, 2)), dma((kv_local, 2, heads)), dma((kv_local, 2, heads)),
            dma((kv_local,)), dma((kv_local, heads)), dma((kv_local, heads)),
            dma((kv_local, levels)), dma((kv_local, levels)),
            dma((kv_local,)), dma((kv_local, heads)), dma((kv_local, heads)),
        ],
        compiler_params=pltpu.CompilerParams(collective_id=0, has_side_effects=True),
        name="attend",
    )(bias, selector, keys, values, queries)


def solution(mesh):
    in_specs = (
        P(("seq", "head"), None),
        P(("seq", "head"), None),
        P(("seq", "head"), None),
        P("head", None),
        P("head"),
        P("seq", None),
        P(),
    )
    out_specs = P(("seq", "head"), None)
    return jax.shard_map(
        on_device, mesh=mesh, in_specs=in_specs, out_specs=out_specs, check_vma=False
    )
```

time: 165 us -> 86.1 us (0.52)
  waiting for transfers between devices: 50.5 us -> 0 us
  Pallas kernels: 38.3 us -> 78.2 us
  starting transfers between devices: 36.4 us -> 0 us
  blocking collectives: 28.7 us -> 0 us
  local copies, waits for them, and re-layouts: 7.85 us -> 4.27 us
    ppermute x16 -> x0, waiting for transfers between devices: 40.3 us -> none  [partner_2(): lax.ppermute(value, axis, [(i, i ^ 1 << stride) for i in range(lax.axis_s...]
    pallas_call x1, Pallas kernels: 38.3 us -> 78.2 us  [on_device(): pl.pallas_call(functools.partial(kernel, heads, levels, kv_local, group),...]
    all_to_all x1 -> x0, blocking collectives: 28.7 us -> none  [on_device(): lax.all_to_all(result, 'head', split_axis=0, concat_axis=1, tiled=True)]
    ppermute x16 -> x0, starting transfers between devices: 24.8 us -> none  [partner_2(): lax.ppermute(value, axis, [(i, i ^ 1 << stride) for i in range(lax.axis_s...]
    all_to_all x3 -> x0, starting transfers between devices: 11.6 us -> none  [the longest x1 4.23 us: on_device(): lax.all_to_all(keys, 'head', split_axis=1, concat_axis=0, tiled=True)]
    all_to_all x3 -> x0, waiting for transfers between devices: 10.3 us -> none  [the longest x1 7.88 us: on_device(): lax.all_to_all(keys, 'head', split_axis=1, concat_axis=0, tiled=True)]
    all_to_all x4 -> x0, local copies, waits for them, and re-layouts: 6 us -> none  [the longest x1 2.02 us: on_device(): lax.all_to_all(keys, 'head', split_axis=1, concat_axis=0, tiled=True)]
    unnamed x18 -> x1, local copies, waits for them, and re-layouts: 1.35 us -> 3.13 us
  transfers between devices with their start and end apart: 19 -> 0, of which waited for: 9 -> 0; matrix products, arithmetic and copies ran while one was open for 3% -> 0% of each run, Pallas kernels for 0% -> 0%
where the time goes in v2:
time: 86.1 us; the launch traced here: 85.9 us
  Pallas kernels  78.2 us (91%)
  local copies, waits for them, and re-layouts  4.27 us (5%)
  other arithmetic  3.38 us (4%)
    pallas_call x1, Pallas kernels, on_device(): pl.pallas_call(functools.partial(kernel, heads, levels, kv_local, group),...  78.2 us
    unnamed x1, local copies, waits for them, and re-layouts  3.13 us

profile of v2, /device:TPU:0, one launch (start us, length us, event | category | flops | bytes accessed | tf_op | source)
XLA Modules:
  0.0 85.9 jit_solution(2238991969726268020)
XLA Ops:
  0.0 0.7 fusion.2
  0.7 0.8 multiply_reduce_fusion
  1.4 0.1 copy.9
  1.5 0.1 copy.11
  1.6 0.1 copy.8
  1.7 0.1 copy.10
  1.8 0.7 copy.12
  2.5 0.1 stack.23
  2.6 0.6 broadcast_multiply_fusion.bias_ref
  3.2 1.3 %compare_convert_fusion.sel_ref = bf16[64,256]{1,0:T(8,128)(2,1)} fusion(s32[256]{0:T(256)S(1)} %iota_add_fusion, s32[64]{0:T(128)} %param.13), kind=kLoop, calls=%fused_computation | loop fusion | flops 32768 | bytes 34048 | tf_op jit(solution)/shard_map/convert_element_type | solution.py:246
  4.5 78.2 %attend.1 = bf16[256,4096]{1,0:T(8,128)(2,1)} custom-call(f32[16,6]{1,0:T(8,128)} %broadcast_multiply_fusion.bias_ref, bf16[64,256]{1,0:T(8,128)(2,1)} %compare_convert_fusion.sel_ref, bf16[256,1024]{1,0:T(8,128)(2,1)} %keys_ref.1, bf16[256,1024]{1,0:T(8,128)(2,1)} %values_ref.1, bf16[256,4096]{1,0:T(8,128)(2,1)} %queries_ref.1), custom_call_target="tpu_custom_call" | custom-call | tf_op jit(solution)/shard_map/attend/pallas_call | solution.py:257
  82.8 3.1 %copy.14 = bf16[256,4096]{1,0:T(8,128)(2,1)} copy(bf16[256,4096]{1,0:T(8,128)(2,1)} %attend.1) | data formatting | bytes 4194304
  (2 shorter events, 0.0 us)

commit v3 on v2

--- a/solution.py
+++ b/solution.py
@@ -33,7 +33,7 @@
 
 def kernel(
     heads, levels, kv_local, group,
-    bias_ref, sel_ref, keys_ref, values_ref, queries_ref, out_ref,
+    level_ref, anchor_ref, partners_ref, places_ref, keys_ref, values_ref, queries_ref, out_ref,
     blocks, qbuf, obuf, part, part_in, carry, carry_in,
     part_send, part_recv, carry_send, carry_recv,
     own_sem, x_send, x_recv, own_q_sem, q_send, q_recv,
@@ -138,12 +138,16 @@
         for c in range(2):
             own_copy(j, c).start()
         own_q(j).start()
+    first = (seat * heads + me) * t
+    places = places_ref[...] - first
+    token = lax.broadcasted_iota(jnp.int32, (places.shape[0], t), 1)
+    selector = jnp.where(places == token, 1.0, 0.0).astype(jnp.bfloat16)
     for d in range(heads):
         for j in range(kv_local):
             for c in range(2):
                 src = (keys_ref, values_ref)[c]
                 part[d, j, c] = jnp.dot(
-                    sel_ref[...], src[:, cols(peer(d), j, HD)], preferred_element_type=jnp.float32
+                    selector, src[:, cols(peer(d), j, HD)], preferred_element_type=jnp.float32
                 ).astype(jnp.bfloat16)
     pl.semaphore_wait(barrier, heads - 1 + levels)
     for d in range(1, heads):
@@ -169,17 +173,24 @@
         send_part(d).wait_recv()
         held = held + part_in[d].astype(jnp.float32)
     carry[levels] = held.astype(jnp.bfloat16)
-    sent = 0
     for l in reversed(range(levels)):
         send_carry(l).start()
-        if sent < kv_local:
-            forward(sent)
-            sent += 1
+        if levels - 1 - l < kv_local:
+            forward(levels - 1 - l)
         send_carry(l).wait_recv()
         carry[l] = (carry[l + 1].astype(jnp.float32) + carry_in[l].astype(jnp.float32)).astype(
             jnp.bfloat16)
-    for j in range(sent, kv_local):
+    for j in range(levels, kv_local):
         forward(j)
+
+    def biases(h):
+        found = [jnp.float32(0.0)]
+        for l in range(levels):
+            total = jnp.float32(0.0)
+            for m in range(levels):
+                total += jnp.where(partners_ref[0, m] == partner(l), level_ref[h, m], 0.0)
+            found.append(total * LOG2E)
+        return found + [anchor_ref[h] * LOG2E]
 
     def one(step, _):
         j = lax.div(step, heads)
@@ -200,7 +211,7 @@
                 qbuf[j, here, g * HD:(g + 1) * HD],
                 [blocks[n, j, 0] for n in range(levels + 1)] + [carry[0, j, 0]],
                 [blocks[n, j, 1] for n in range(levels + 1)] + [carry[0, j, 1]],
-                [bias_ref[j * group + g, n] for n in range(levels + 2)],
+                biases(j * group + g),
                 scale,
             )
             obuf[j, d, :, g * HD:(g + 1) * HD] = result.astype(jnp.bfloat16)
@@ -240,23 +251,14 @@
     kv_local = keys.shape[1] // HD // heads
     group = level_bias.shape[0] // kv_local
     anchors = anchor_positions.shape[0]
-    block_index = lax.axis_index("seq")
-    first = (block_index * heads + lax.axis_index("head")) * t
-    token_index = first + jnp.arange(t, dtype=jnp.int32)
-    selector = (anchor_positions[:, None] == token_index[None, :]).astype(jnp.bfloat16)
-    biases = [jnp.zeros_like(anchor_bias)]
-    for l in range(levels):
-        chosen = (partners[0] == jnp.bitwise_xor(block_index, 1 << l)).astype(jnp.float32)
-        biases.append(jnp.sum(level_bias * chosen[None, :], axis=1))
-    biases.append(anchor_bias)
-    bias = jnp.stack(biases, axis=1) * LOG2E
+    smem = pl.BlockSpec(memory_space=pltpu.SMEM)
     vmem = pl.BlockSpec(memory_space=pltpu.VMEM)
     dma = pltpu.SemaphoreType.DMA
     anchor_shape = (kv_local, 2, anchors, HD)
     bf16 = jnp.bfloat16
     return pl.pallas_call(
         functools.partial(kernel, heads, levels, kv_local, group),
-        in_specs=[pl.BlockSpec(memory_space=pltpu.SMEM), vmem, vmem, vmem,
+        in_specs=[smem, smem, smem, vmem, vmem, vmem,
                   pl.BlockSpec(memory_space=pl.ANY)],
         out_specs=pl.BlockSpec(memory_space=pl.ANY),
         out_shape=jax.ShapeDtypeStruct(queries.shape, queries.dtype),
@@ -276,7 +278,7 @@
         ],
         compiler_params=pltpu.CompilerParams(collective_id=0, has_side_effects=True),
         name="attend",
-    )(bias, selector, keys, values, queries)
+    )(level_bias, anchor_bias, partners, anchor_positions[:, None], keys, values, queries)
 
 
 def solution(mesh):

time: 86.1 us -> 84.4 us (0.980)
  other arithmetic: 3.38 us -> 0 us
  local copies, waits for them, and re-layouts: 4.27 us -> 5.84 us
    broadcast_in_dim x0 -> x1, local copies, waits for them, and re-layouts: none -> 1.36 us  [on_device(): anchor_positions[:, None]]
    unnamed x1 -> x2, local copies, waits for them, and re-layouts: 3.13 us -> 4.48 us
    convert_element_type x1 -> x0, other arithmetic: 1.35 us -> none  [on_device(): (anchor_positions[:, None] == token_index[None, :]).astype(jnp.bfloat16)]
    mul x2 -> x0, other arithmetic: 1.26 us -> none  [the longest x1 0.66 us: on_device(): biases.append(jnp.sum(level_bias * chosen[None, :], axis=1))]
    another operation x7 -> x0, local copies, waits for them, and re-layouts: 1.14 us -> none  [the longest x6 1.14 us: on_device(): bias = jnp.stack(biases, axis=1) * LOG2E]
where the time goes in v3:
time: 84.4 us; the launch traced here: 84.2 us
  Pallas kernels  78.4 us (93%)
  local copies, waits for them, and re-layouts  5.84 us (7%)
    pallas_call x1, Pallas kernels, on_device(): pl.pallas_call(functools.partial(kernel, heads, levels, kv_local, group),...  78.4 us
    unnamed x2, local copies, waits for them, and re-layouts  4.48 us

profile of v3, /device:TPU:0, one launch (start us, length us, event | category | flops | bytes accessed | tf_op | source)
XLA Modules:
  0.0 84.2 jit_solution(16161751010593163050)
XLA Ops:
  0.0 1.4 %copy.8.level_ref = f32[16,4]{1,0:T(8,128)} copy(f32[16,4]{0,1:T(4,128)} %param.10) | data formatting | bytes 512 | tf_op args[3]
  1.4 1.4 %copy.9.places_ref = s32[64,1]{1,0:T(8,128)} copy(s32[64,1]{0,1:T(1,128)} %bitcast.1) | data formatting | bytes 512 | tf_op jit(solution)/shard_map/broadcast_in_dim | solution.py:281
  2.7 78.4 %attend.1 = bf16[256,4096]{1,0:T(8,128)(2,1)} custom-call(f32[16,4]{1,0:T(8,128)} %copy.8.level_ref, f32[16]{0:T(128)} %anchor_ref.1, s32[1,4]{1,0:T(1,128)} %partners_ref.1, s32[64,1]{1,0:T(8,128)} %copy.9.places_ref, bf16[256,1024]{1,0:T(8,128)(2,1)} %keys_ref.1, bf16[256,1024]{1,0:T(8,128)(2,1)} %values_ref.1, bf16[256,4096]{1,0:T(8,128)(2,1)} %queries_ref.1), custom_call_target="tpu_custom_call" | custom-call | tf_op jit(solution)/shard_map/attend/pallas_call | solution.py:259
  81.1 3.1 %copy.11 = bf16[256,4096]{1,0:T(8,128)(2,1)} copy(bf16[256,4096]{1,0:T(8,128)(2,1)} %attend.1) | data formatting | bytes 4194304
